TPU v7x, 32 devices: a whole 2x2x4 slice. The times are simulated.
32 devices in a mesh: tile: 8 (over y, x, core), depth: 4 (over z).
Axes of the slice: x: 2, y: 2, z: 4, core: 2. Of those that a mesh axis runs over, the one named last changes fastest.
Arguments:
- patches: float32 [512, 256, 256], P('tile', 'depth'), may hold values from -6 to 6
- patch_owner: int32 [512, 1], P('tile'), may hold values from 0 to 7; in each aligned block of 64 rows (0 to 63, 64 to 127, ...) at most 8 rows name the same one
- patch_level: int32 [512], P('tile'), may hold values from 0 to 63
- phases: float32 [512, 256, 256], P('tile', None, 'depth'), may hold values from -3.140625 to 3.140625
Outputs:
- intensity: float32 [512, 256, 256], P('tile', 'depth')
Inputs may be any that keep to these rules, and one draw needn't show every extreme that they name: `patch_owner`: among the 64 patches of one index of tile, at most 8 have the same owner.
All inputs are finite; a program needn't handle non-finite values.
Results may differ from a plain program's by a relative error of at most 0.00017.
Values sent between devices are 32-bit elements; how exact they have to be, the bound alone decides.
No kernel may reach another device: no remote copies, remote signals or barrier semaphores. Data moves between devices by JAX's collectives and lax.ppermute only.
A program may use at most 128 MiB of HBM per device.

v0:
```python
import math

import jax
import jax.numpy as jnp
from jax import lax
from jax.sharding import PartitionSpec as P

CAP = 8


HIGHEST_PRECISION = lax.Precision.HIGHEST


def tables(extent):
    indices = jnp.arange(extent, dtype=jnp.int32)
    product = indices[:, None] * indices[None, :] % extent
    angles = product.astype(jnp.float32) * (2.0 * math.pi / extent)
    return (jnp.cos(angles), jnp.sin(angles))


def right_apply(values, matrix):
    return jnp.einsum(
        "src,ck->srk",
        values,
        matrix,
        precision=HIGHEST_PRECISION,
        preferred_element_type=jnp.float32,
    )


def apply_rows(matrix, values):
    return jnp.einsum(
        "jk,skc->sjc",
        matrix,
        values,
        precision=HIGHEST_PRECISION,
        preferred_element_type=jnp.float32,
    )


def refocus_local(field, phase):
    extent = field.shape[2]
    cosine_table, sine_table = tables(extent)
    real_gain = jnp.cos(phase)
    imag_gain = jnp.sin(phase)
    col_real = right_apply(field, cosine_table)
    col_imag = -right_apply(field, sine_table)
    spec_real = apply_rows(cosine_table, col_real) + apply_rows(sine_table, col_imag)
    spec_imag = apply_rows(cosine_table, col_imag) - apply_rows(sine_table, col_real)
    prop_real = spec_real * real_gain - spec_imag * imag_gain
    prop_imag = spec_real * imag_gain + spec_imag * real_gain
    back_real = apply_rows(cosine_table, prop_real) - apply_rows(sine_table, prop_imag)
    back_imag = apply_rows(cosine_table, prop_imag) + apply_rows(sine_table, prop_real)
    field_real = right_apply(back_real, cosine_table) - right_apply(back_imag, sine_table)
    field_imag = right_apply(back_real, sine_table) + right_apply(back_imag, cosine_table)
    return (field_real * field_real + field_imag * field_imag) * (1.0 / float(extent) ** 4)


def on_device(patches, patch_owner, patch_level, phases):
    patch_count, row_count, extent = patches.shape
    levels = phases.shape[0]
    owners = lax.axis_size("tile")
    owner_column = patch_owner[:, 0]
    level_hot = (patch_level[:, None] == jnp.arange(levels, dtype=jnp.int32)[None, :]).astype(
        jnp.float32
    )
    owner_hot = (owner_column[:, None] == jnp.arange(owners, dtype=jnp.int32)[None, :]).astype(
        jnp.float32
    )
    before = jnp.tril(jnp.ones((patch_count, patch_count), jnp.float32), -1)
    rank_value = jnp.sum(
        jnp.dot(before, owner_hot, precision=HIGHEST_PRECISION, preferred_element_type=jnp.float32)
        * owner_hot,
        axis=1,
    )
    slot_index = owner_column * CAP + rank_value.astype(jnp.int32)
    slot_count = owners * CAP
    slot_hot = (jnp.arange(slot_count, dtype=jnp.int32)[:, None] == slot_index[None, :]).astype(
        jnp.float32
    )
    outgoing = jnp.dot(
        slot_hot,
        patches.reshape(patch_count, -1),
        precision=HIGHEST_PRECISION,
        preferred_element_type=jnp.float32,
    )
    outgoing = outgoing.reshape(slot_count, row_count, extent)
    chosen = jnp.dot(
        slot_hot, level_hot, precision=HIGHEST_PRECISION, preferred_element_type=jnp.float32
    )
    incoming, picked = (
        lax.all_to_all(outgoing, "tile", split_axis=0, concat_axis=0, tiled=True),
        lax.all_to_all(chosen, "tile", split_axis=0, concat_axis=0, tiled=True),
    )
    flattened = phases.reshape(levels, -1)
    phase_rows = jnp.dot(
        picked, flattened, precision=HIGHEST_PRECISION, preferred_element_type=jnp.float32
    )
    phase_rows = phase_rows.reshape(slot_count, phases.shape[1], phases.shape[2])
    phase_turned = jnp.transpose(phase_rows, (0, 2, 1))
    whole_field, whole_phase = (
        lax.all_to_all(incoming, "depth", split_axis=0, concat_axis=1, tiled=True),
        lax.all_to_all(phase_turned, "depth", split_axis=0, concat_axis=1, tiled=True),
    )
    local_result = refocus_local(whole_field, jnp.transpose(whole_phase, (0, 2, 1)))
    result = lax.all_to_all(local_result, "depth", split_axis=1, concat_axis=0, tiled=True)
    returned = lax.all_to_all(result, "tile", split_axis=0, concat_axis=0, tiled=True)
    placed = jnp.dot(
        slot_hot.T,
        returned.reshape(slot_count, -1),
        precision=HIGHEST_PRECISION,
        preferred_element_type=jnp.float32,
    )
    return placed.reshape(patch_count, row_count, extent)


def solution(mesh):
    return jax.shard_map(
        on_device,
        mesh=mesh,
        in_specs=(P("tile", "depth", None), P("tile", None), P("tile"), P("tile", None, "depth")),
        out_specs=P("tile", "depth", None),
        check_vma=False,
    )
```

profile of v0, /device:TPU:0, one launch (start us, length us, event | category | flops | bytes accessed | tf_op | source)
XLA Modules:
  0.0 528.9 jit_solution(16689904573134012535)
XLA Ops:
  0.0 0.9 fusion.42
  1.0 0.7 convert_add_fusion
  1.6 0.9 convolution_bitcast_fusion.1
  2.6 0.7 reshape.39
  3.2 5.2 all-to-all-start.2
  8.4 6.9 %fusion.3 = f32[64,64,256]{2,0,1:T(8,128)S(1)} fusion(s32[64]{0:T(128)S(1)} %convert_add_fusion, f32[8,8,64,256]{3,2,1,0:T(8,128)} %bitcast.140), kind=kOutput, calls=%fused_computation.3 | convolution fusion | flops 805310464 | bytes 8388864 | tf_op jit(solution)/shard_map/dot_general | solution.py:81
  15.3 4.4 copy.58
  19.7 0.0 all-to-all-done.2
  19.7 4.8 all-to-all-start
  24.5 6.9 %copy.62 = f32[64,256,64]{2,1,0:T(8,128)} copy(f32[64,256,64]{1,2,0:T(8,128)} %param.7) | data formatting | bytes 8388608 | tf_op args[3]
  31.4 6.9 %reshape.32 = f32[64,16384]{1,0:T(8,128)} reshape(f32[64,256,64]{2,1,0:T(8,128)} %copy.62) | data formatting | bytes 8388608 | tf_op jit(solution)/shard_map/reshape | solution.py:95
  38.3 7.4 %dot_general.79 = f32[256,64,64]{1,0,2:T(8,128)} reshape(f32[16384,64]{0,1:T(8,128)} %bitcast.134) | data formatting | bytes 8388608 | tf_op jit(solution)/shard_map/dot_general | solution.py:96
  45.6 7.3 %copy.63 = f32[256,64,64]{0,2,1:T(8,128)} copy(f32[256,64,64]{1,0,2:T(8,128)} %dot_general.79) | data formatting | bytes 8388608 | tf_op jit(solution)/shard_map/dot_general | solution.py:96
  52.9 0.5 broadcast.68
  53.5 0.6 reduce
  54.1 0.1 reshape.40
  54.2 5.5 %convolution_bitcast_fusion = f32[64,64,256]{2,0,1:T(8,128)S(1)} fusion(f32[256,64,64]{0,2,1:T(8,128)} %copy.63, f32[8,8,64]{2,1,0:T(8,128)S(1)} %reshape.40), kind=kOutput, calls=%fused_computation.33 | convolution fusion | flops 805306368 | bytes 8404992 | tf_op jit(solution)/shard_map/dot_general | solution.py:96
  59.7 4.4 copy.64
  64.1 9.5 %all-to-all-done = f32[64,64,256]{2,1,0:T(8,128)} async-done(((f32[64,64,256]{2,1,0:T(8,128)}), f32[64,64,256]{2,1,0:T(8,128)}, u32[]{:S(2)}, u32[]{:S(2)}) %all-to-all-start) | async-done | bytes 4194336 | tf_op jit(solution)/shard_map/all_to_all | solution.py:92
  73.6 96.2 %all_to_all.67 = f32[64,64,256]{2,1,0:T(8,128)} all-to-all(f32[64,64,256]{2,1,0:T(8,128)} %copy.64), channel_id=1, replica_groups=mesh['tile'=8,'depth'=4] {'depth'}, dimensions={0} | all-to-all | bytes 8388608 | tf_op jit(solution)/shard_map/all_to_all | solution.py:103
  169.8 4.8 all-to-all-start.1
  174.7 16.0 %fusion.154 = (f32[64,64,256]{2,1,0:T(8,128)S(1)}, f32[64,64,256]{2,1,0:T(8,128)S(1)}) fusion(f32[64,64,256]{2,1,0:T(8,128)} %all_to_all.67), kind=kLoop, calls=%fused_computation.145 | loop fusion | bytes 12582912 | tf_op jit(solution)/shard_map/sin | solution.py:45
  190.6 2.3 copy.65
  192.9 2.3 copy.68
  195.2 71.0 %all-to-all-done.1 = f32[64,64,256]{2,1,0:T(8,128)} async-done(((f32[64,64,256]{2,1,0:T(8,128)}), f32[64,64,256]{2,1,0:T(8,128)}, u32[]{:S(2)}, u32[]{:S(2)}) %all-to-all-start.1) | async-done | bytes 4194336 | tf_op jit(solution)/shard_map/all_to_all | solution.py:102
  266.2 2.5 copy.59
  268.7 5.2 fusion.62
  273.9 4.6 fusion.53
  278.4 5.0 fusion.50
  283.5 6.9 %fusion.60 = f32[16,256,256]{2,1,0:T(8,128)} fusion(f32[16,256,256]{1,2,0:T(8,128)S(1)} %fusion.62), kind=kOutput, calls=%fused_computation.61 | convolution fusion | flops 3222142976 | bytes 8388608 | tf_op jit(solution)/shard_map/jk,skc->sjc/dot_general | solution.py:32
  290.4 0.0 copy-start
  290.4 8.2 %fusion.31 = f32[16,256,256]{2,1,0:T(8,128)S(1)} fusion(f32[16,256,256]{2,1,0:T(8,128)S(1)} %fusion.50, f32[16,256,256]{2,1,0:T(8,128)S(1)} %fusion.53), kind=kOutput, calls=%fused_computation.35 | convolution fusion | flops 3224240128 | bytes 12582912 | tf_op jit(solution)/shard_map/jk,skc->sjc/dot_general | solution.py:32
  298.6 0.0 copy-done
  298.6 13.1 %fusion.18 = (f32[16,256,256]{2,1,0:T(8,128)S(1)}, f32[16,256,256]{2,1,0:T(8,128)S(1)}) fusion(f32[4,16,64,256]{3,2,0,1:T(8,128)S(1)} %copy-done, f32[16,256,256]{2,1,0:T(8,128)S(1)} %fusion.31, f32[4,16,64,256]{3,2,0,1:T(8,128)} %copy.68, f32[16,256,256]{2,1,0:T(8,128)} %fusion.60, f32[16,256,256]{2,1,0:T(8,128)S(1)} %fusion.53), kind=kOutput, calls=%fused_computation.20 | convolution fusion | flops 3230531584 | bytes 29360128 | tf_op jit(solution)/shard_map/jk,skc->sjc/dot_general | solution.py:32
  311.7 4.8 fusion.16
  316.5 4.4 fusion.14
  320.9 4.4 fusion.37
  325.3 8.4 %fusion.6 = f32[16,256,256]{2,1,0:T(8,128)S(1)} fusion(f32[16,256,256]{2,1,0:T(8,128)S(1)} %fusion.37), kind=kOutput, calls=%fused_computation.6 | convolution fusion | flops 3222142976 | bytes 8388608 | tf_op jit(solution)/shard_map/src,ck->srk/dot_general | solution.py:22
  333.7 8.2 %fusion.8 = f32[16,256,256]{2,1,0:T(8,128)S(1)} fusion(f32[16,256,256]{2,1,0:T(8,128)S(1)} %fusion.37), kind=kOutput, calls=%fused_computation.8 | convolution fusion | flops 3222142976 | bytes 8388608 | tf_op jit(solution)/shard_map/src,ck->srk/dot_general | solution.py:22
  342.0 4.8 fusion.34
  346.7 8.3 %fusion.10 = f32[16,256,256]{2,1,0:T(8,128)S(1)} fusion(f32[16,256,256]{2,1,0:T(8,128)S(1)} %fusion.34), kind=kOutput, calls=%fused_computation.10 | convolution fusion | flops 3222142976 | bytes 8388608 | tf_op jit(solution)/shard_map/src,ck->srk/dot_general | solution.py:22
  355.0 8.8 %add_multiply_fusion = f32[16,256,256]{2,1,0:T(8,128)S(1)} fusion(f32[16,256,256]{2,1,0:T(8,128)S(1)} %fusion.10, f32[16,256,256]{2,1,0:T(8,128)S(1)} %fusion.6, f32[16,256,256]{2,1,0:T(8,128)S(1)} %fusion.8, f32[16,256,256]{2,1,0:T(8,128)S(1)} %fusion.34), kind=kOutput, calls=%fused_computation.28 | convolution fusion | flops 3228434432 | bytes 20971520 | tf_op jit(solution)/shard_map/src,ck->srk/dot_general | solution.py:22
  363.8 2.7 copy.73
  366.5 95.3 %all_to_all.68 = f32[16,256,256]{2,0,1:T(8,128)S(1)} all-to-all(f32[16,256,256]{2,0,1:T(8,128)S(1)} %copy.73), channel_id=1, replica_groups=mesh['tile'=8,'depth'=4] {'depth'}, dimensions={1} | all-to-all | bytes 8388608 | tf_op jit(solution)/shard_map/all_to_all | solution.py:106
  461.8 2.4 copy.75
  464.2 55.0 %all_to_all.69 = f32[64,64,256]{2,1,0:T(8,128)S(1)} all-to-all(f32[64,64,256]{2,1,0:T(8,128)S(1)} %bitcast.139), channel_id=1, replica_groups=mesh['tile'=8,'depth'=4] {'tile'}, dimensions={0} | all-to-all | bytes 8388608 | tf_op jit(solution)/shard_map/all_to_all | solution.py:107
  519.2 4.8 fusion
  524.0 4.4 copy.77
  (1 shorter events, 0.0 us)
Async XLA Ops:
  3.2 16.5 %all-to-all-start.2 = ((f32[8,1,512]{2,1,0:T(1,128)}), f32[8,1,512]{2,1,0:T(1,128)S(1)}, u32[]{:S(2)}, u32[]{:S(2)}) async-start(f32[8,1,512]{2,1,0:T(1,128)} %reshape.39), calls=%async_computation.2 | async-start | bytes 32768 | tf_op jit(solution)/shard_map/all_to_all | solution.py:93
  19.7 53.9 %all-to-all-start = ((f32[64,64,256]{2,1,0:T(8,128)}), f32[64,64,256]{2,1,0:T(8,128)}, u32[]{:S(2)}, u32[]{:S(2)}) async-start(f32[64,64,256]{2,1,0:T(8,128)} %copy.58), calls=%async_computation | async-start | bytes 8388608 | tf_op jit(solution)/shard_map/all_to_all | solution.py:92
  169.8 96.4 %all-to-all-start.1 = ((f32[64,64,256]{2,1,0:T(8,128)}), f32[64,64,256]{2,1,0:T(8,128)}, u32[]{:S(2)}, u32[]{:S(2)}) async-start(f32[64,64,256]{2,1,0:T(8,128)} %all-to-all-done), calls=%async_computation.1 | async-start | bytes 8388608 | tf_op jit(solution)/shard_map/all_to_all | solution.py:102
  290.4 8.2 %copy-start = (f32[4,16,64,256]{3,2,0,1:T(8,128)S(1)}, f32[4,16,64,256]{3,2,0,1:T(8,128)}, u32[]{:S(2)}) copy-start(f32[4,16,64,256]{3,2,0,1:T(8,128)} %copy.65) | copy-start | bytes 12582916
where the time goes:
time: 535 us; the launch traced here: 529 us
  blocking collectives  246 us (46%)
  matrix products  114 us (21%)
  waiting for transfers between devices  80.5 us (15%)
  local copies, waits for them, and re-layouts  71.1 us (13%)
  starting transfers between devices  14.8 us (3%)
    all_to_all x1, blocking collectives, on_device(): lax.all_to_all(phase_turned, 'depth', split_axis=0, concat_axis=1, tiled=...  96.2 us
    all_to_all x1, blocking collectives, on_device(): lax.all_to_all(local_result, 'depth', split_axis=1, concat_axis=0, tiled=...  95.3 us
    all_to_all x1, waiting for transfers between devices, on_device(): lax.all_to_all(incoming, 'depth', split_axis=0, concat_axis=1, tiled=True)  71 us
    all_to_all x1, blocking collectives, on_device(): lax.all_to_all(result, 'tile', split_axis=0, concat_axis=0, tiled=True)  55 us
    dot_general x8, matrix products, apply_rows(): jnp.einsum('jk,skc->sjc', matrix, values, precision=HIGHEST_PRECISION, pr...  51.6 us
    dot_general x6, matrix products, right_apply(): jnp.einsum('src,ck->srk', values, matrix, precision=HIGHEST_PRECISION, pr...  43.4 us
    sin x2, local copies, waits for them, and re-layouts, refocus_local(): imag_gain = jnp.sin(phase)  18.2 us
    dot_general x2, local copies, waits for them, and re-layouts, on_device(): jnp.dot(picked, flattened, precision=HIGHEST_PRECISION, preferred_element...  14.7 us
  transfers between devices with their start and end apart: 3, of which 2 were waited for; matrix products, arithmetic and copies ran while one was open for 13% of the time, Pallas kernels for 0%

commit v1 on v0

v1 whole, which is shorter than its diff:
```python
import functools
import math

import jax
import jax.numpy as jnp
import numpy as np
from jax import lax
from jax.experimental import pallas as pl
from jax.experimental.pallas import tpu as pltpu
from jax.sharding import PartitionSpec as P

CAP = 8


def split(values):
    high = values.astype(jnp.bfloat16)
    low = (values - high.astype(jnp.float32)).astype(jnp.bfloat16)
    return high, low


def tables(extent):
    index = np.arange(extent)
    angles = (index[:, None] * index[None, :] % extent) * (2.0 * math.pi / extent)
    parts = []
    for table in (np.cos(angles), np.sin(angles)):
        table = table.astype(np.float32)
        high = table.astype(jnp.bfloat16)
        parts += [high, (table - high.astype(np.float32)).astype(jnp.bfloat16)]
    return np.stack(parts)


def sincos(angle):
    half = angle * 0.5
    square = half * half
    sine = jnp.float32(-1.0 / math.factorial(11))
    for power, sign in ((9, 1.0), (7, -1.0), (5, 1.0), (3, -1.0), (1, 1.0)):
        sine = sine * square + jnp.float32(sign / math.factorial(power))
    sine = sine * half
    cosine = jnp.float32(1.0 / math.factorial(12))
    for power, sign in ((10, -1.0), (8, 1.0), (6, -1.0), (4, 1.0), (2, -1.0), (0, 1.0)):
        cosine = cosine * square + jnp.float32(sign / math.factorial(power))
    return 2.0 * sine * cosine, 1.0 - 2.0 * sine * sine


def product(left, right, contract):
    dims = (contract, ((), ()))
    dot = functools.partial(
        lax.dot_general, dimension_numbers=dims, preferred_element_type=jnp.float32
    )
    return dot(left[0], right[0]) + (dot(left[0], right[1]) + dot(left[1], right[0]))


NN = ((1,), (0,))
NT = ((1,), (1,))


def refocus_kernel(table_ref, field_ref, phase_ref, out_ref, left_ref, right_ref):
    extent = table_ref.shape[1]

    @pl.when(pl.program_id(0) == 0)
    def _():
        for part in range(2):
            cosine, sine = table_ref[part], table_ref[2 + part]
            left_ref[part, :extent, :extent] = cosine
            left_ref[part, :extent, extent:] = -sine
            left_ref[part, extent:, :extent] = sine
            left_ref[part, extent:, extent:] = cosine
            right_ref[part, :extent, :extent] = cosine
            right_ref[part, :extent, extent:] = sine
            right_ref[part, extent:, :extent] = -sine
            right_ref[part, extent:, extent:] = cosine

    left = (left_ref[0], left_ref[1])
    right = (right_ref[0], right_ref[1])
    patch = field_ref[...].reshape(extent, extent)
    half_turned = product(
        (left_ref[0, :, :extent], left_ref[1, :, :extent]), split(patch), NT
    )
    half_turned = jnp.concatenate([half_turned[:extent], half_turned[extent:]], axis=1)
    spectrum = product(split(half_turned), right, NN)
    spec_real, spec_negated = spectrum[:, :extent], spectrum[:, extent:]
    sine, cosine = sincos(phase_ref[...].reshape(extent, extent))
    prop_real = spec_real * cosine + spec_negated * sine
    prop_imag = spec_real * sine - spec_negated * cosine
    propagated = jnp.concatenate([prop_real, prop_imag], axis=1)
    back = product(left, split(propagated), NT)
    back = jnp.concatenate([back[:extent], back[extent:]], axis=1)
    field = product(split(back), right, NN)
    field_real, field_imag = field[:, :extent], field[:, extent:]
    intensity = (field_real * field_real + field_imag * field_imag) * (1.0 / float(extent) ** 4)
    out_ref[...] = intensity.reshape(out_ref.shape)


def refocus(field, phase, phase_slot_first):
    parts, slots, rows, extent = field.shape
    if phase_slot_first:
        phase_block, phase_map = (1,) + phase.shape[1:], lambda i: (i, 0, 0, 0)
    else:
        phase_block, phase_map = phase.shape[:1] + (1,) + phase.shape[2:], lambda i: (0, i, 0, 0)
    field_spec = pl.BlockSpec((parts, 1, rows, extent), lambda i: (0, i, 0, 0))
    return pl.pallas_call(
        refocus_kernel,
        grid=(slots,),
        in_specs=[
            pl.BlockSpec((4, extent, extent), lambda i: (0, 0, 0)),
            field_spec,
            pl.BlockSpec(phase_block, phase_map),
        ],
        out_specs=field_spec,
        out_shape=jax.ShapeDtypeStruct(field.shape, jnp.float32),
        scratch_shapes=[pltpu.VMEM((2, 2 * extent, 2 * extent), jnp.bfloat16)] * 2,
        name="refocus",
    )(jnp.asarray(tables(extent)), field, phase)


def gather_kernel(index_ref, source_ref, out_ref, sems):
    count = out_ref.shape[0]

    def copy(i):
        return pltpu.make_async_copy(source_ref.at[index_ref[i]], out_ref.at[i], sems.at[i])

    def start(i, _):
        copy(i).start()
        return _

    def wait(i, _):
        copy(i).wait()
        return _

    lax.fori_loop(0, count, start, 0)
    lax.fori_loop(0, count, wait, 0)


def gather(index, source):
    count = index.shape[0]
    return pl.pallas_call(
        gather_kernel,
        grid_spec=pltpu.PrefetchScalarGridSpec(
            num_scalar_prefetch=1,
            in_specs=[pl.BlockSpec(memory_space=pl.ANY)],
            out_specs=pl.BlockSpec(memory_space=pl.ANY),
            scratch_shapes=[pltpu.SemaphoreType.DMA((count,))],
        ),
        out_shape=jax.ShapeDtypeStruct((count,) + source.shape[1:], source.dtype),
        name="gather_blocks",
    )(index, source)


def scatter_kernel(filled, *refs):
    index_ref, source_ref, out_ref, sems = refs[0], refs[1], refs[-2], refs[-1]
    count = source_ref.shape[0]

    def each(act):
        def step(i, _):
            place = index_ref[i]
            if filled:
                act(pltpu.make_async_copy(source_ref.at[i], out_ref.at[place], sems.at[i]))
            else:
                @pl.when(place >= 0)
                def _():
                    act(pltpu.make_async_copy(source_ref.at[i], out_ref.at[place], sems.at[i]))
            return 0

        lax.fori_loop(0, count, step, 0)

    each(lambda copy: copy.start())
    each(lambda copy: copy.wait())


def scatter(index, source, into, out_shape, filled):
    count = source.shape[0]
    anywhere = pl.BlockSpec(memory_space=pl.ANY)
    operands = (source,) if into is None else (source, into)
    return pl.pallas_call(
        functools.partial(scatter_kernel, filled),
        grid_spec=pltpu.PrefetchScalarGridSpec(
            num_scalar_prefetch=1,
            in_specs=[anywhere] * len(operands),
            out_specs=anywhere,
            scratch_shapes=[pltpu.SemaphoreType.DMA((count,))],
        ),
        out_shape=jax.ShapeDtypeStruct(out_shape, source.dtype),
        input_output_aliases={} if into is None else {2: 0},
        name="scatter_blocks",
    )(index, *operands)


def on_device(patches, patch_owner, patch_level, phases):
    patch_count, row_count, extent = patches.shape
    owners = lax.axis_size("tile")
    parts = lax.axis_size("depth")
    slot_count = owners * CAP
    filled = slot_count == patch_count
    direct = CAP % parts == 0
    owner = patch_owner[:, 0]
    numbers = jnp.arange(patch_count, dtype=jnp.int32)
    rank = jnp.sum(
        (owner[:, None] == owner[None, :]) & (numbers[None, :] < numbers[:, None]),
        axis=1,
        dtype=jnp.int32,
    )
    slot = owner * CAP + rank
    slot_hot = jnp.arange(slot_count, dtype=jnp.int32)[:, None] == slot[None, :]
    level_of_slot = jnp.sum(jnp.where(slot_hot, patch_level[None, :], 0), axis=1, dtype=jnp.int32)
    patch_of_slot = jnp.sum(jnp.where(slot_hot, numbers[None, :] + 1, 0), axis=1, dtype=jnp.int32) - 1
    wanted = lax.all_to_all(
        level_of_slot.reshape(owners, CAP), "tile", split_axis=0, concat_axis=0, tiled=True
    )
    turned = jnp.transpose(phases, (0, 2, 1))
    columns = turned.shape[1]
    chunks = CAP // parts if direct else 1
    result = None
    for chunk in range(chunks):
        if direct:
            order = patch_of_slot.reshape(owners, parts, chunks)[:, :, chunk].T.reshape(-1)
            levels = wanted.reshape(owners, parts, chunks)[:, :, chunk].reshape(-1)
        else:
            order, levels = patch_of_slot, wanted.reshape(-1)
        sent = gather(order if filled else jnp.maximum(order, 0), patches)
        field = lax.all_to_all(sent, "depth", split_axis=0, concat_axis=0, tiled=True)
        field = field.reshape(parts, -1, row_count, extent)
        picked = gather(levels, turned)
        if direct:
            phase = lax.all_to_all(
                picked, ("tile", "depth"), split_axis=0, concat_axis=0, tiled=True
            ).reshape(owners, parts, columns, extent)
        else:
            picked = lax.all_to_all(picked, "tile", split_axis=0, concat_axis=0, tiled=True)
            phase = lax.all_to_all(
                picked, "depth", split_axis=0, concat_axis=0, tiled=True
            ).reshape(parts, -1, columns, extent)
        local = refocus(field, phase, direct)
        back = lax.all_to_all(
            local.reshape(-1, row_count, extent), "depth", split_axis=0, concat_axis=0, tiled=True
        )
        result = scatter(order, back, result, patches.shape, filled)
    return result


def solution(mesh):
    return jax.shard_map(
        on_device,
        mesh=mesh,
        in_specs=(P("tile", "depth", None), P("tile", None), P("tile"), P("tile", None, "depth")),
        out_specs=P("tile", "depth", None),
        check_vma=False,
    )
```

time: 535 us -> 536 us (level); the launches traced: 529 us -> 535 us
  Pallas kernels: 0 us -> 447 us
  blocking collectives: 246 us -> 0 us
  matrix products: 114 us -> 0 us
  local copies, waits for them, and re-layouts: 71.1 us -> 6.55 us
  waiting for transfers between devices: 80.5 us -> 42.8 us
  starting transfers between devices: 14.8 us -> 37 us
    pallas_call x0 -> x8, Pallas kernels: none -> 447 us  [the longest x4 262 us: gather(): pl.pallas_call(gather_kernel, grid_spec=pltpu.PrefetchScalarGridSpec(num_...]
    all_to_all x3 -> x0, blocking collectives: 246 us -> none  [the longest x1 96.2 us: on_device(): lax.all_to_all(phase_turned, 'depth', split_axis=0, concat_axis=1, tiled=...]
    dot_general x19 -> x0, matrix products: 114 us -> none  [the longest x8 51.6 us: apply_rows(): jnp.einsum('jk,skc->sjc', matrix, values, precision=HIGHEST_PRECISION, pr...]
    all_to_all x3 -> x7, waiting for transfers between devices: 80.5 us -> 42.8 us  [the longest x2 22.5 us: on_device(): lax.all_to_all(local.reshape(-1, row_count, extent), 'depth', split_axis=...]
    dot_general x4 -> x0, local copies, waits for them, and re-layouts: 23.5 us -> none  [the longest x2 14.7 us: on_device(): jnp.dot(picked, flattened, precision=HIGHEST_PRECISION, preferred_element...]
    all_to_all x3 -> x7, starting transfers between devices: 14.8 us -> 37 us  [the longest x2 12.5 us: on_device(): lax.all_to_all(picked, ('tile', 'depth'), split_axis=0, concat_axis=0, ti...]
    sin x2 -> x0, local copies, waits for them, and re-layouts: 18.2 us -> none  [refocus_local(): imag_gain = jnp.sin(phase)]
    reshape x1 -> x2, local copies, waits for them, and re-layouts: 6.87 us -> 1.23 us  [on_device(): patch_of_slot.reshape(owners, parts, chunks)[:, :, chunk].T.reshape(-1)]
  transfers between devices with their start and end apart: 3 -> 7, of which waited for: 2 -> 2; matrix products, arithmetic and copies ran while one was open for 13% -> 1% of each run, Pallas kernels for 0% -> 71%
where the time goes in v1:
time: 536 us; the launch traced here: 535 us
  Pallas kernels  447 us (83%)
  waiting for transfers between devices  42.8 us (8%)
  starting transfers between devices  37 us (7%)
  local copies, waits for them, and re-layouts  6.55 us (1%)
    pallas_call x4, Pallas kernels, gather(): pl.pallas_call(gather_kernel, grid_spec=pltpu.PrefetchScalarGridSpec(num_...  262 us
    pallas_call x2, Pallas kernels, scatter(): pl.pallas_call(functools.partial(scatter_kernel, filled), grid_spec=pltpu...  131 us
    pallas_call x2, Pallas kernels, refocus(): pl.pallas_call(refocus_kernel, grid=(slots,), in_specs=[pl.BlockSpec((4,...  53.1 us
    all_to_all x2, waiting for transfers between devices, on_device(): lax.all_to_all(local.reshape(-1, row_count, extent), 'depth', split_axis=...  22.5 us
    all_to_all x2, waiting for transfers between devices, on_device(): lax.all_to_all(picked, ('tile', 'depth'), split_axis=0, concat_axis=0, ti...  20.3 us
    all_to_all x2, starting transfers between devices, on_device(): lax.all_to_all(picked, ('tile', 'depth'), split_axis=0, concat_axis=0, ti...  12.5 us
  transfers between devices with their start and end apart: 7, of which 2 were waited for; matrix products, arithmetic and copies ran while one was open for 1% of the time, Pallas kernels for 71%

profile of v1, /device:TPU:0, one launch (start us, length us, event | category | flops | bytes accessed | tf_op | source)
XLA Modules:
  0.0 535.4 jit_solution(14459848577084846870)
XLA Ops:
  0.0 0.9 convert_reduce_fusion
  0.9 0.7 iota_add_fusion
  1.6 0.8 select_reduce_fusion
  2.3 0.7 all_to_all.25
  3.0 5.2 all-to-all-start.1
  8.2 0.1 sub.7
  8.3 0.1 fusion.1
  8.4 0.1 copy.24
  8.5 0.6 reshape.53.index_ref.refs_0_
  9.2 65.6 %gather_blocks.4 = f32[32,64,256]{2,1,0:T(8,128)} custom-call(s32[32]{0:T(128)} %reshape.53.index_ref.refs_0_, f32[64,64,256]{2,1,0:T(8,128)} %source_ref.3), custom_call_target="tpu_custom_call" | custom-call | tf_op jit(solution)/shard_map/gather_blocks/pallas_call | solution.py:136
  74.8 0.0 all-to-all-done.1
  74.8 4.9 all-to-all-start
  79.6 0.1 copy.28
  79.8 0.6 reshape.58.index_ref.refs_0_
  80.3 65.6 %gather_blocks.6 = f32[32,64,256]{2,1,0:T(8,128)} custom-call(s32[32]{0:T(128)} %reshape.58.index_ref.refs_0_, f32[64,64,256]{2,1,0:T(8,128)} %source_ref.3), custom_call_target="tpu_custom_call" | custom-call | tf_op jit(solution)/shard_map/gather_blocks/pallas_call | solution.py:136
  145.9 0.0 all-to-all-done
  145.9 0.0 copy-start.1
  146.0 5.1 all-to-all-start.4
  151.1 0.1 copy.26
  151.1 0.0 copy-done.1
  151.1 0.1 copy.29
  151.2 0.7 reshape_squeeze.7.index_ref
  151.9 65.6 %gather_blocks.7 = f32[32,64,256]{2,1,0:T(8,128)} custom-call(s32[32]{0:T(128)} %reshape_squeeze.7.index_ref, f32[64,64,256]{2,1,0:T(8,128)} %bitcast.21), custom_call_target="tpu_custom_call" | custom-call | tf_op jit(solution)/shard_map/gather_blocks/pallas_call | solution.py:136
  217.5 0.0 all-to-all-done.4
  217.5 6.6 %all-to-all-start.5 = ((f32[32,64,256]{2,1,0:T(8,128)}), f32[32,64,256]{2,1,0:T(8,128)S(1)}, u32[]{:S(2)}, u32[]{:S(2)}) async-start(f32[32,64,256]{2,1,0:T(8,128)} %gather_blocks.7), calls=%async_computation.5 | async-start | bytes 4194304 | tf_op jit(solution)/shard_map/all_to_all | solution.py:224
  224.0 0.1 copy.27
  224.1 0.7 reshape_squeeze.6.index_ref
  224.8 65.6 %gather_blocks.5 = f32[32,64,256]{2,1,0:T(8,128)} custom-call(s32[32]{0:T(128)} %reshape_squeeze.6.index_ref, f32[64,64,256]{2,1,0:T(8,128)} %bitcast.22), custom_call_target="tpu_custom_call" | custom-call | tf_op jit(solution)/shard_map/gather_blocks/pallas_call | solution.py:136
  290.4 0.0 all-to-all-done.5
  290.4 0.0 copy-start.2
  290.4 1.4 copy-done.2
  291.7 6.0 %all-to-all-start.2 = ((f32[32,64,256]{2,1,0:T(8,128)}), f32[32,64,256]{2,1,0:T(8,128)}, u32[]{:S(2)}, u32[]{:S(2)}) async-start(f32[32,64,256]{2,1,0:T(8,128)} %gather_blocks.5), calls=%async_computation.2 | async-start | bytes 4194304 | tf_op jit(solution)/shard_map/all_to_all | solution.py:224
  297.7 26.6 %refocus.3 = f32[4,8,64,256]{3,2,1,0:T(8,128)} custom-call(bf16[4,256,256]{2,1,0:T(8,128)(2,1)} %constant.11.clone.table_ref, f32[4,8,64,256]{3,2,1,0:T(8,128)} %bitcast.11.field_ref, f32[8,4,64,256]{3,2,1,0:T(8,128)} %bitcast.24), custom_call_target="tpu_custom_call" | custom-call | tf_op jit(solution)/shard_map/refocus/pallas_call | solution.py:101
  324.3 20.3 %all-to-all-done.2 = f32[32,64,256]{2,1,0:T(8,128)} async-done(((f32[32,64,256]{2,1,0:T(8,128)}), f32[32,64,256]{2,1,0:T(8,128)}, u32[]{:S(2)}, u32[]{:S(2)}) %all-to-all-start.2) | async-done | bytes 2097184 | tf_op jit(solution)/shard_map/all_to_all | solution.py:224
  344.6 4.9 all-to-all-start.6
  349.5 26.5 %refocus.2 = f32[4,8,64,256]{3,2,1,0:T(8,128)} custom-call(bf16[4,256,256]{2,1,0:T(8,128)(2,1)} %constant.11.clone.table_ref, f32[4,8,64,256]{3,2,1,0:T(8,128)} %bitcast.23, f32[8,4,64,256]{3,2,1,0:T(8,128)} %bitcast.7.phase_ref), custom_call_target="tpu_custom_call" | custom-call | tf_op jit(solution)/shard_map/refocus/pallas_call | solution.py:101
  376.0 22.5 %all-to-all-done.6.refs_1_ = f32[32,64,256]{2,1,0:T(8,128)S(1)} async-done(((f32[32,64,256]{2,1,0:T(8,128)}), f32[32,64,256]{2,1,0:T(8,128)S(1)}, u32[]{:S(2)}, u32[]{:S(2)}) %all-to-all-start.6) | async-done | bytes 2097184 | tf_op jit(solution)/shard_map/all_to_all | solution.py:233
  398.5 0.0 copy-start
  398.5 1.3 copy-done
  399.8 4.5 all-to-all-start.3
  404.3 65.6 %scatter_blocks.2.refs_2_ = f32[64,64,256]{2,1,0:T(8,128)} custom-call(s32[32]{0:T(128)} %reshape.58.index_ref.refs_0_, f32[32,64,256]{2,1,0:T(8,128)} %copy-done), custom_call_target="tpu_custom_call" | custom-call | tf_op jit(solution)/shard_map/scatter_blocks/pallas_call | solution.py:174
  469.9 0.0 all-to-all-done.3.refs_1_
  469.9 65.6 %scatter_blocks.3 = f32[64,64,256]{2,1,0:T(8,128)} custom-call(s32[32]{0:T(128)} %reshape.53.index_ref.refs_0_, f32[32,64,256]{2,1,0:T(8,128)} %all-to-all-done.3.refs_1_, f32[64,64,256]{2,1,0:T(8,128)} %scatter_blocks.2.refs_2_), custom_call_target="tpu_custom_call", output_to_operand_aliasing={{}: (2, {})} | custom-call | tf_op jit(solution)/shard_map/scatter_blocks/pallas_call | solution.py:174
  (2 shorter events, 0.0 us)
Async XLA Ops:
  3.0 71.7 %all-to-all-start.1 = ((s32[8,1,8]{2,1,0:T(1,128)}), s32[8,1,8]{2,1,0:T(1,128)S(1)}, u32[]{:S(2)}, u32[]{:S(2)}) async-start(s32[8,1,8]{2,1,0:T(1,128)} %bitcast.4), calls=%async_computation.1 | async-start | bytes 8192 | tf_op jit(solution)/shard_map/all_to_all | solution.py:206
  74.8 71.2 %all-to-all-start = ((f32[32,64,256]{2,1,0:T(8,128)}), f32[32,64,256]{2,1,0:T(8,128)S(1)}, u32[]{:S(2)}, u32[]{:S(2)}) async-start(f32[32,64,256]{2,1,0:T(8,128)} %gather_blocks.4), calls=%async_computation | async-start | bytes 4194304 | tf_op jit(solution)/shard_map/all_to_all | solution.py:220
  145.9 5.2 copy-start.1
  146.0 71.5 %all-to-all-start.4 = ((f32[32,64,256]{2,1,0:T(8,128)}), f32[32,64,256]{2,1,0:T(8,128)}, u32[]{:S(2)}, u32[]{:S(2)}) async-start(f32[32,64,256]{2,1,0:T(8,128)} %gather_blocks.6), calls=%async_computation.4 | async-start | bytes 4194304 | tf_op jit(solution)/shard_map/all_to_all | solution.py:220
  217.5 72.9 %all-to-all-start.5 = ((f32[32,64,256]{2,1,0:T(8,128)}), f32[32,64,256]{2,1,0:T(8,128)S(1)}, u32[]{:S(2)}, u32[]{:S(2)}) async-start(f32[32,64,256]{2,1,0:T(8,128)} %gather_blocks.7), calls=%async_computation.5 | async-start | bytes 4194304 | tf_op jit(solution)/shard_map/all_to_all | solution.py:224
  290.4 1.4 copy-start.2
  291.7 52.8 %all-to-all-start.2 = ((f32[32,64,256]{2,1,0:T(8,128)}), f32[32,64,256]{2,1,0:T(8,128)}, u32[]{:S(2)}, u32[]{:S(2)}) async-start(f32[32,64,256]{2,1,0:T(8,128)} %gather_blocks.5), calls=%async_computation.2 | async-start | bytes 4194304 | tf_op jit(solution)/shard_map/all_to_all | solution.py:224
  344.6 53.9 %all-to-all-start.6 = ((f32[32,64,256]{2,1,0:T(8,128)}), f32[32,64,256]{2,1,0:T(8,128)S(1)}, u32[]{:S(2)}, u32[]{:S(2)}) async-start(f32[32,64,256]{2,1,0:T(8,128)} %bitcast.25), calls=%async_computation.6 | async-start | bytes 4194304 | tf_op jit(solution)/shard_map/all_to_all | solution.py:233
  398.5 1.3 copy-start
  399.8 70.1 %all-to-all-start.3 = ((f32[32,64,256]{2,1,0:T(8,128)}), f32[32,64,256]{2,1,0:T(8,128)}, u32[]{:S(2)}, u32[]{:S(2)}) async-start(f32[32,64,256]{2,1,0:T(8,128)} %bitcast.26), calls=%async_computation.3 | async-start | bytes 4194304 | tf_op jit(solution)/shard_map/all_to_all | solution.py:233

commit v2 on v1

--- a/solution.py
+++ b/solution.py
@@ -113,76 +113,64 @@
     )(jnp.asarray(tables(extent)), field, phase)
 
 
-def gather_kernel(index_ref, source_ref, out_ref, sems):
-    count = out_ref.shape[0]
-
-    def copy(i):
-        return pltpu.make_async_copy(source_ref.at[index_ref[i]], out_ref.at[i], sems.at[i])
-
-    def start(i, _):
-        copy(i).start()
-        return _
-
-    def wait(i, _):
-        copy(i).wait()
-        return _
-
-    lax.fori_loop(0, count, start, 0)
-    lax.fori_loop(0, count, wait, 0)
-
-
-def gather(index, source):
+def move_kernel(scatter, filled, *refs):
+    index_ref, source_ref, out_ref, held, come, gone = refs[0], refs[1], *refs[-4:]
+    count = held.shape[0]
+
+    def guarded(place, act):
+        if filled:
+            act()
+        else:
+            pl.when(place >= 0)(act)
+
+    def each(act):
+        def step(i, carry):
+            guarded(index_ref[i], lambda: act(i))
+            return carry
+
+        lax.fori_loop(0, count, step, 0)
+
+    def fetch(i):
+        block = source_ref.at[i if scatter else index_ref[i]]
+        return pltpu.make_async_copy(block, held.at[i], come.at[i])
+
+    def store(i):
+        block = out_ref.at[index_ref[i] if scatter else i]
+        return pltpu.make_async_copy(held.at[i], block, gone.at[i])
+
+    def pass_on(i):
+        fetch(i).wait()
+        store(i).start()
+
+    each(lambda i: fetch(i).start())
+    each(pass_on)
+    each(lambda i: store(i).wait())
+
+
+def move(index, source, out_shape, scatter, filled, into=None):
     count = index.shape[0]
-    return pl.pallas_call(
-        gather_kernel,
-        grid_spec=pltpu.PrefetchScalarGridSpec(
-            num_scalar_prefetch=1,
-            in_specs=[pl.BlockSpec(memory_space=pl.ANY)],
-            out_specs=pl.BlockSpec(memory_space=pl.ANY),
-            scratch_shapes=[pltpu.SemaphoreType.DMA((count,))],
-        ),
-        out_shape=jax.ShapeDtypeStruct((count,) + source.shape[1:], source.dtype),
-        name="gather_blocks",
-    )(index, source)
-
-
-def scatter_kernel(filled, *refs):
-    index_ref, source_ref, out_ref, sems = refs[0], refs[1], refs[-2], refs[-1]
-    count = source_ref.shape[0]
-
-    def each(act):
-        def step(i, _):
-            place = index_ref[i]
-            if filled:
-                act(pltpu.make_async_copy(source_ref.at[i], out_ref.at[place], sems.at[i]))
-            else:
-                @pl.when(place >= 0)
-                def _():
-                    act(pltpu.make_async_copy(source_ref.at[i], out_ref.at[place], sems.at[i]))
-            return 0
-
-        lax.fori_loop(0, count, step, 0)
-
-    each(lambda copy: copy.start())
-    each(lambda copy: copy.wait())
-
-
-def scatter(index, source, into, out_shape, filled):
-    count = source.shape[0]
     anywhere = pl.BlockSpec(memory_space=pl.ANY)
     operands = (source,) if into is None else (source, into)
     return pl.pallas_call(
-        functools.partial(scatter_kernel, filled),
+        functools.partial(move_kernel, scatter, filled),
         grid_spec=pltpu.PrefetchScalarGridSpec(
             num_scalar_prefetch=1,
             in_specs=[anywhere] * len(operands),
             out_specs=anywhere,
-            scratch_shapes=[pltpu.SemaphoreType.DMA((count,))],
+            scratch_shapes=[
+                pltpu.VMEM((count,) + source.shape[1:], source.dtype),
+                pltpu.SemaphoreType.DMA((count,)),
+                pltpu.SemaphoreType.DMA((count,)),
+            ],
         ),
         out_shape=jax.ShapeDtypeStruct(out_shape, source.dtype),
         input_output_aliases={} if into is None else {2: 0},
-        name="scatter_blocks",
+        name="scatter_blocks" if scatter else "gather_blocks",
     )(index, *operands)
+
+
+def gather(index, source, filled):
+    return move(index, source, index.shape + source.shape[1:], False, filled)
 
 
 def on_device(patches, patch_owner, patch_level, phases):
@@ -216,10 +204,10 @@
             levels = wanted.reshape(owners, parts, chunks)[:, :, chunk].reshape(-1)
         else:
             order, levels = patch_of_slot, wanted.reshape(-1)
-        sent = gather(order if filled else jnp.maximum(order, 0), patches)
+        sent = gather(order, patches, filled)
         field = lax.all_to_all(sent, "depth", split_axis=0, concat_axis=0, tiled=True)
         field = field.reshape(parts, -1, row_count, extent)
-        picked = gather(levels, turned)
+        picked = gather(levels, turned, True)
         if direct:
             phase = lax.all_to_all(
                 picked, ("tile", "depth"), split_axis=0, concat_axis=0, tiled=True
@@ -233,7 +221,7 @@
         back = lax.all_to_all(
             local.reshape(-1, row_count, extent), "depth", split_axis=0, concat_axis=0, tiled=True
         )
-        result = scatter(order, back, result, patches.shape, filled)
+        result = move(order, back, patches.shape, True, filled, result)
     return result
 
 

time: 536 us -> 335 us (0.62)
  Pallas kernels: 447 us -> 74.8 us
  waiting for transfers between devices: 42.8 us -> 217 us
    pallas_call x6, Pallas kernels: 393 us -> 21.7 us  [move(): pl.pallas_call(functools.partial(move_kernel, scatter, filled), grid_spec...]
    all_to_all x2, waiting for transfers between devices: 0.01 us -> 87.4 us  [on_device(): lax.all_to_all(sent, 'depth', split_axis=0, concat_axis=0, tiled=True)]
    all_to_all x2, waiting for transfers between devices: 22.5 us -> 67.2 us  [on_device(): lax.all_to_all(local.reshape(-1, row_count, extent), 'depth', split_axis=...]
    all_to_all x2, waiting for transfers between devices: 20.3 us -> 62.4 us  [on_device(): lax.all_to_all(picked, ('tile', 'depth'), split_axis=0, concat_axis=0, ti...]
  transfers between devices with their start and end apart: 7 -> 7, of which waited for: 2 -> 7; matrix products, arithmetic and copies ran while one was open for 1% -> 1% of each run, Pallas kernels for 71% -> 21%
where the time goes in v2:
time: 335 us; the launch traced here: 334 us
  waiting for transfers between devices  217 us (65%)
  Pallas kernels  74.8 us (22%)
  starting transfers between devices  32.6 us (10%)
  local copies, waits for them, and re-layouts  6.55 us (2%)
    all_to_all x2, waiting for transfers between devices, on_device(): lax.all_to_all(sent, 'depth', split_axis=0, concat_axis=0, tiled=True)  87.4 us
    all_to_all x2, waiting for transfers between devices, on_device(): lax.all_to_all(local.reshape(-1, row_count, extent), 'depth', split_axis=...  67.2 us
    all_to_all x2, waiting for transfers between devices, on_device(): lax.all_to_all(picked, ('tile', 'depth'), split_axis=0, concat_axis=0, ti...  62.4 us
    pallas_call x2, Pallas kernels, refocus(): pl.pallas_call(refocus_kernel, grid=(slots,), in_specs=[pl.BlockSpec((4,...  53.1 us
    pallas_call x6, Pallas kernels, move(): pl.pallas_call(functools.partial(move_kernel, scatter, filled), grid_spec...  21.7 us
    all_to_all x2, starting transfers between devices, on_device(): lax.all_to_all(local.reshape(-1, row_count, extent), 'depth', split_axis=...  9.54 us
    all_to_all x2, starting transfers between devices, on_device(): lax.all_to_all(sent, 'depth', split_axis=0, concat_axis=0, tiled=True)  9.33 us
    all_to_all x2, starting transfers between devices, on_device(): lax.all_to_all(picked, ('tile', 'depth'), split_axis=0, concat_axis=0, ti...  8.49 us
  transfers between devices with their start and end apart: 7, of which 7 were waited for; matrix products, arithmetic and copies ran while one was open for 1% of the time, Pallas kernels for 21%

profile of v2, /device:TPU:0, one launch (start us, length us, event | category | flops | bytes accessed | tf_op | source)
XLA Modules:
  0.0 333.7 jit_solution(4598480127971958515)
XLA Ops:
  0.0 0.9 convert_reduce_fusion
  0.9 0.7 iota_add_fusion
  1.6 0.8 select_reduce_fusion
  2.3 0.7 all_to_all.25
  3.0 5.2 %all-to-all-start.1 = ((s32[8,1,8]{2,1,0:T(1,128)}), s32[8,1,8]{2,1,0:T(1,128)S(1)}, u32[]{:S(2)}, u32[]{:S(2)}) async-start(s32[8,1,8]{2,1,0:T(1,128)} %bitcast.4), calls=%async_computation.1 | async-start | bytes 8192 | tf_op jit(solution)/shard_map/all_to_all | solution.py:194
  8.2 0.1 sub.7
  8.3 0.1 fusion.1
  8.4 0.1 copy.24
  8.5 0.6 reshape.53.refs_0_
  9.2 3.5 %gather_blocks.4 = f32[32,64,256]{2,1,0:T(8,128)} custom-call(s32[32]{0:T(128)} %reshape.53.refs_0_, f32[64,64,256]{2,1,0:T(8,128)} %refs_1_.3), custom_call_target="tpu_custom_call" | custom-call | tf_op jit(solution)/shard_map/gather_blocks/pallas_call | solution.py:154
  12.6 0.3 all-to-all-done.1
  12.9 4.9 %all-to-all-start = ((f32[32,64,256]{2,1,0:T(8,128)}), f32[32,64,256]{2,1,0:T(8,128)S(1)}, u32[]{:S(2)}, u32[]{:S(2)}) async-start(f32[32,64,256]{2,1,0:T(8,128)} %gather_blocks.4), calls=%async_computation | async-start | bytes 4194304 | tf_op jit(solution)/shard_map/all_to_all | solution.py:208
  17.8 0.1 copy.28
  17.9 0.6 reshape.58.refs_0_
  18.5 3.5 %gather_blocks.6 = f32[32,64,256]{2,1,0:T(8,128)} custom-call(s32[32]{0:T(128)} %reshape.58.refs_0_, f32[64,64,256]{2,1,0:T(8,128)} %refs_1_.3), custom_call_target="tpu_custom_call" | custom-call | tf_op jit(solution)/shard_map/gather_blocks/pallas_call | solution.py:154
  22.0 44.4 %all-to-all-done = f32[32,64,256]{2,1,0:T(8,128)S(1)} async-done(((f32[32,64,256]{2,1,0:T(8,128)}), f32[32,64,256]{2,1,0:T(8,128)S(1)}, u32[]{:S(2)}, u32[]{:S(2)}) %all-to-all-start) | async-done | bytes 2097184 | tf_op jit(solution)/shard_map/all_to_all | solution.py:208
  66.4 0.0 copy-start.1
  66.4 4.5 %all-to-all-start.4 = ((f32[32,64,256]{2,1,0:T(8,128)}), f32[32,64,256]{2,1,0:T(8,128)}, u32[]{:S(2)}, u32[]{:S(2)}) async-start(f32[32,64,256]{2,1,0:T(8,128)} %gather_blocks.6), calls=%async_computation.4 | async-start | bytes 4194304 | tf_op jit(solution)/shard_map/all_to_all | solution.py:208
  70.9 0.1 copy.26
  70.9 0.0 copy-done.1
  70.9 0.1 copy.29
  71.0 0.7 reshape_squeeze.7.refs_0_
  71.7 4.0 %gather_blocks.7 = f32[32,64,256]{2,1,0:T(8,128)} custom-call(s32[32]{0:T(128)} %reshape_squeeze.7.refs_0_, f32[64,64,256]{2,1,0:T(8,128)} %bitcast.21), custom_call_target="tpu_custom_call" | custom-call | tf_op jit(solution)/shard_map/gather_blocks/pallas_call | solution.py:154
  75.7 43.0 %all-to-all-done.4 = f32[32,64,256]{2,1,0:T(8,128)} async-done(((f32[32,64,256]{2,1,0:T(8,128)}), f32[32,64,256]{2,1,0:T(8,128)}, u32[]{:S(2)}, u32[]{:S(2)}) %all-to-all-start.4) | async-done | bytes 2097184 | tf_op jit(solution)/shard_map/all_to_all | solution.py:208
  118.7 3.8 %all-to-all-start.5 = ((f32[32,64,256]{2,1,0:T(8,128)}), f32[32,64,256]{2,1,0:T(8,128)S(1)}, u32[]{:S(2)}, u32[]{:S(2)}) async-start(f32[32,64,256]{2,1,0:T(8,128)} %gather_blocks.7), calls=%async_computation.5 | async-start | bytes 4194304 | tf_op jit(solution)/shard_map/all_to_all | solution.py:212
  122.5 0.1 copy.27
  122.6 0.7 reshape_squeeze.6.refs_0_
  123.2 3.8 %gather_blocks.5 = f32[32,64,256]{2,1,0:T(8,128)} custom-call(s32[32]{0:T(128)} %reshape_squeeze.6.refs_0_, f32[64,64,256]{2,1,0:T(8,128)} %bitcast.22), custom_call_target="tpu_custom_call" | custom-call | tf_op jit(solution)/shard_map/gather_blocks/pallas_call | solution.py:154
  127.0 42.3 %all-to-all-done.5 = f32[32,64,256]{2,1,0:T(8,128)S(1)} async-done(((f32[32,64,256]{2,1,0:T(8,128)}), f32[32,64,256]{2,1,0:T(8,128)S(1)}, u32[]{:S(2)}, u32[]{:S(2)}) %all-to-all-start.5) | async-done | bytes 2097184 | tf_op jit(solution)/shard_map/all_to_all | solution.py:212
  169.4 0.0 copy-start.2
  169.4 1.4 copy-done.2
  170.7 4.7 %all-to-all-start.2 = ((f32[32,64,256]{2,1,0:T(8,128)}), f32[32,64,256]{2,1,0:T(8,128)}, u32[]{:S(2)}, u32[]{:S(2)}) async-start(f32[32,64,256]{2,1,0:T(8,128)} %gather_blocks.5), calls=%async_computation.2 | async-start | bytes 4194304 | tf_op jit(solution)/shard_map/all_to_all | solution.py:212
  175.4 26.6 %refocus.3 = f32[4,8,64,256]{3,2,1,0:T(8,128)} custom-call(bf16[4,256,256]{2,1,0:T(8,128)(2,1)} %constant.11.clone.table_ref, f32[4,8,64,256]{3,2,1,0:T(8,128)} %bitcast.11.field_ref, f32[8,4,64,256]{3,2,1,0:T(8,128)} %bitcast.24), custom_call_target="tpu_custom_call" | custom-call | tf_op jit(solution)/shard_map/refocus/pallas_call | solution.py:101
  202.0 20.1 %all-to-all-done.2 = f32[32,64,256]{2,1,0:T(8,128)} async-done(((f32[32,64,256]{2,1,0:T(8,128)}), f32[32,64,256]{2,1,0:T(8,128)}, u32[]{:S(2)}, u32[]{:S(2)}) %all-to-all-start.2) | async-done | bytes 2097184 | tf_op jit(solution)/shard_map/all_to_all | solution.py:212
  222.1 5.1 %all-to-all-start.6 = ((f32[32,64,256]{2,1,0:T(8,128)}), f32[32,64,256]{2,1,0:T(8,128)S(1)}, u32[]{:S(2)}, u32[]{:S(2)}) async-start(f32[32,64,256]{2,1,0:T(8,128)} %bitcast.25), calls=%async_computation.6 | async-start | bytes 4194304 | tf_op jit(solution)/shard_map/all_to_all | solution.py:221
  227.2 26.5 %refocus.2 = f32[4,8,64,256]{3,2,1,0:T(8,128)} custom-call(bf16[4,256,256]{2,1,0:T(8,128)(2,1)} %constant.11.clone.table_ref, f32[4,8,64,256]{3,2,1,0:T(8,128)} %bitcast.23, f32[8,4,64,256]{3,2,1,0:T(8,128)} %bitcast.7.phase_ref), custom_call_target="tpu_custom_call" | custom-call | tf_op jit(solution)/shard_map/refocus/pallas_call | solution.py:101
  253.7 22.5 %all-to-all-done.6.refs_1_ = f32[32,64,256]{2,1,0:T(8,128)S(1)} async-done(((f32[32,64,256]{2,1,0:T(8,128)}), f32[32,64,256]{2,1,0:T(8,128)S(1)}, u32[]{:S(2)}, u32[]{:S(2)}) %all-to-all-start.6) | async-done | bytes 2097184 | tf_op jit(solution)/shard_map/all_to_all | solution.py:221
  276.2 0.0 copy-start
  276.2 1.3 copy-done
  277.5 4.5 %all-to-all-start.3 = ((f32[32,64,256]{2,1,0:T(8,128)}), f32[32,64,256]{2,1,0:T(8,128)}, u32[]{:S(2)}, u32[]{:S(2)}) async-start(f32[32,64,256]{2,1,0:T(8,128)} %bitcast.26), calls=%async_computation.3 | async-start | bytes 4194304 | tf_op jit(solution)/shard_map/all_to_all | solution.py:221
  282.0 3.5 %scatter_blocks.2.refs_2_ = f32[64,64,256]{2,1,0:T(8,128)} custom-call(s32[32]{0:T(128)} %reshape.58.refs_0_, f32[32,64,256]{2,1,0:T(8,128)} %copy-done), custom_call_target="tpu_custom_call" | custom-call | tf_op jit(solution)/shard_map/scatter_blocks/pallas_call | solution.py:154
  285.5 44.7 %all-to-all-done.3.refs_1_ = f32[32,64,256]{2,1,0:T(8,128)} async-done(((f32[32,64,256]{2,1,0:T(8,128)}), f32[32,64,256]{2,1,0:T(8,128)}, u32[]{:S(2)}, u32[]{:S(2)}) %all-to-all-start.3) | async-done | bytes 2097184 | tf_op jit(solution)/shard_map/all_to_all | solution.py:221
  330.2 3.5 %scatter_blocks.3 = f32[64,64,256]{2,1,0:T(8,128)} custom-call(s32[32]{0:T(128)} %reshape.53.refs_0_, f32[32,64,256]{2,1,0:T(8,128)} %all-to-all-done.3.refs_1_, f32[64,64,256]{2,1,0:T(8,128)} %scatter_blocks.2.refs_2_), custom_call_target="tpu_custom_call", output_to_operand_aliasing={{}: (2, {})} | custom-call | tf_op jit(solution)/shard_map/scatter_blocks/pallas_call | solution.py:154
  (2 shorter events, 0.0 us)
Async XLA Ops:
  3.0 9.9 %all-to-all-start.1 = ((s32[8,1,8]{2,1,0:T(1,128)}), s32[8,1,8]{2,1,0:T(1,128)S(1)}, u32[]{:S(2)}, u32[]{:S(2)}) async-start(s32[8,1,8]{2,1,0:T(1,128)} %bitcast.4), calls=%async_computation.1 | async-start | bytes 8192 | tf_op jit(solution)/shard_map/all_to_all | solution.py:194
  12.9 53.5 %all-to-all-start = ((f32[32,64,256]{2,1,0:T(8,128)}), f32[32,64,256]{2,1,0:T(8,128)S(1)}, u32[]{:S(2)}, u32[]{:S(2)}) async-start(f32[32,64,256]{2,1,0:T(8,128)} %gather_blocks.4), calls=%async_computation | async-start | bytes 4194304 | tf_op jit(solution)/shard_map/all_to_all | solution.py:208
  66.4 4.5 %copy-start.1 = (f32[32,64,256]{2,1,0:T(8,128)}, f32[32,64,256]{2,1,0:T(8,128)S(1)}, u32[]{:S(2)}) copy-start(f32[32,64,256]{2,1,0:T(8,128)S(1)} %all-to-all-done) | copy-start | bytes 6291460
  66.4 52.3 %all-to-all-start.4 = ((f32[32,64,256]{2,1,0:T(8,128)}), f32[32,64,256]{2,1,0:T(8,128)}, u32[]{:S(2)}, u32[]{:S(2)}) async-start(f32[32,64,256]{2,1,0:T(8,128)} %gather_blocks.6), calls=%async_computation.4 | async-start | bytes 4194304 | tf_op jit(solution)/shard_map/all_to_all | solution.py:208
  118.7 50.7 %all-to-all-start.5 = ((f32[32,64,256]{2,1,0:T(8,128)}), f32[32,64,256]{2,1,0:T(8,128)S(1)}, u32[]{:S(2)}, u32[]{:S(2)}) async-start(f32[32,64,256]{2,1,0:T(8,128)} %gather_blocks.7), calls=%async_computation.5 | async-start | bytes 4194304 | tf_op jit(solution)/shard_map/all_to_all | solution.py:212
  169.4 1.4 copy-start.2
  170.7 51.4 %all-to-all-start.2 = ((f32[32,64,256]{2,1,0:T(8,128)}), f32[32,64,256]{2,1,0:T(8,128)}, u32[]{:S(2)}, u32[]{:S(2)}) async-start(f32[32,64,256]{2,1,0:T(8,128)} %gather_blocks.5), calls=%async_computation.2 | async-start | bytes 4194304 | tf_op jit(solution)/shard_map/all_to_all | solution.py:212
  222.1 54.1 %all-to-all-start.6 = ((f32[32,64,256]{2,1,0:T(8,128)}), f32[32,64,256]{2,1,0:T(8,128)S(1)}, u32[]{:S(2)}, u32[]{:S(2)}) async-start(f32[32,64,256]{2,1,0:T(8,128)} %bitcast.25), calls=%async_computation.6 | async-start | bytes 4194304 | tf_op jit(solution)/shard_map/all_to_all | solution.py:221
  276.2 1.3 copy-start
  277.5 52.7 %all-to-all-start.3 = ((f32[32,64,256]{2,1,0:T(8,128)}), f32[32,64,256]{2,1,0:T(8,128)}, u32[]{:S(2)}, u32[]{:S(2)}) async-start(f32[32,64,256]{2,1,0:T(8,128)} %bitcast.26), calls=%async_computation.3 | async-start | bytes 4194304 | tf_op jit(solution)/shard_map/all_to_all | solution.py:221

commit v3 on v2

--- a/solution.py
+++ b/solution.py
@@ -8,6 +8,7 @@
 from jax.experimental import pallas as pl
 from jax.experimental.pallas import tpu as pltpu
 from jax.sharding import PartitionSpec as P
+
 
 CAP = 8
 
@@ -54,7 +55,14 @@
 NT = ((1,), (1,))
 
 
-def refocus_kernel(table_ref, field_ref, phase_ref, out_ref, left_ref, right_ref):
+def rotated(step, parts, rows):
+    part = lax.rem(lax.axis_index("depth") + (step + parts), parts)
+    return pl.ds(pl.multiple_of(part * rows, rows), rows)
+
+
+def refocus_kernel(pieces, table_ref, *refs):
+    field_refs, phase_ref, out_refs = refs[:pieces], refs[pieces], refs[pieces + 1 : 2 * pieces + 1]
+    left_ref, right_ref, whole_ref = refs[2 * pieces + 1 :]
     extent = table_ref.shape[1]
 
     @pl.when(pl.program_id(0) == 0)
@@ -72,7 +80,12 @@
 
     left = (left_ref[0], left_ref[1])
     right = (right_ref[0], right_ref[1])
-    patch = field_ref[...].reshape(extent, extent)
+    if pieces == 1:
+        patch = field_refs[0][...].reshape(extent, extent)
+    else:
+        for step, ref in enumerate(field_refs):
+            whole_ref[rotated(-step, pieces, ref.shape[1]), :] = ref[0]
+        patch = whole_ref[...]
     half_turned = product(
         (left_ref[0, :, :extent], left_ref[1, :, :extent]), split(patch), NT
     )
@@ -88,29 +101,36 @@
     field = product(split(back), right, NN)
     field_real, field_imag = field[:, :extent], field[:, extent:]
     intensity = (field_real * field_real + field_imag * field_imag) * (1.0 / float(extent) ** 4)
-    out_ref[...] = intensity.reshape(out_ref.shape)
-
-
-def refocus(field, phase, phase_slot_first):
-    parts, slots, rows, extent = field.shape
-    if phase_slot_first:
-        phase_block, phase_map = (1,) + phase.shape[1:], lambda i: (i, 0, 0, 0)
+    if pieces == 1:
+        out_refs[0][...] = intensity.reshape(out_refs[0].shape)
     else:
-        phase_block, phase_map = phase.shape[:1] + (1,) + phase.shape[2:], lambda i: (0, i, 0, 0)
-    field_spec = pl.BlockSpec((parts, 1, rows, extent), lambda i: (0, i, 0, 0))
-    return pl.pallas_call(
-        refocus_kernel,
+        whole_ref[...] = intensity
+        for step, ref in enumerate(out_refs):
+            ref[0] = whole_ref[rotated(step, pieces, ref.shape[1]), :]
+
+
+def refocus(fields, phase):
+    pieces, extent = len(fields), phase.shape[-1]
+    if pieces == 1:
+        parts, slots, rows, _ = fields[0].shape
+        field_spec = pl.BlockSpec((parts, 1, rows, extent), lambda i: (0, i, 0, 0))
+        phase_spec = pl.BlockSpec((parts, 1) + phase.shape[2:], lambda i: (0, i, 0, 0))
+    else:
+        slots, rows, _ = fields[0].shape
+        field_spec = pl.BlockSpec((1, rows, extent), lambda i: (i, 0, 0))
+        phase_spec = pl.BlockSpec((1,) + phase.shape[1:], lambda i: (i, 0, 0, 0))
+    return pl.pallas_call(
+        functools.partial(refocus_kernel, pieces),
         grid=(slots,),
-        in_specs=[
-            pl.BlockSpec((4, extent, extent), lambda i: (0, 0, 0)),
-            field_spec,
-            pl.BlockSpec(phase_block, phase_map),
-        ],
-        out_specs=field_spec,
-        out_shape=jax.ShapeDtypeStruct(field.shape, jnp.float32),
-        scratch_shapes=[pltpu.VMEM((2, 2 * extent, 2 * extent), jnp.bfloat16)] * 2,
+        in_specs=[pl.BlockSpec((4, extent, extent), lambda i: (0, 0, 0))]
+        + [field_spec] * pieces
+        + [phase_spec],
+        out_specs=[field_spec] * pieces,
+        out_shape=[jax.ShapeDtypeStruct(fields[0].shape, jnp.float32)] * pieces,
+        scratch_shapes=[pltpu.VMEM((2, 2 * extent, 2 * extent), jnp.bfloat16)] * 2
+        + [pltpu.VMEM((extent, extent), jnp.float32)],
         name="refocus",
-    )(jnp.asarray(tables(extent)), field, phase)
+    )(jnp.asarray(tables(extent)), *fields, phase)
 
 
 def move_kernel(scatter, filled, *refs):
@@ -169,17 +189,276 @@
     )(index, *operands)
 
 
-def gather(index, source, filled):
-    return move(index, source, index.shape + source.shape[1:], False, filled)
-
-
-def on_device(patches, patch_owner, patch_level, phases):
-    patch_count, row_count, extent = patches.shape
-    owners = lax.axis_size("tile")
-    parts = lax.axis_size("depth")
+def loop(count, act):
+    def step(i, carry):
+        act(i)
+        return carry
+
+    lax.fori_loop(0, count, step, 0)
+
+
+def guard(always, condition, act):
+    if always:
+        act()
+    else:
+        pl.when(condition)(act)
+
+
+def step_of(part, parts):
+    return lax.rem(part - lax.axis_index("depth") + parts, parts)
+
+
+def route_kernel(filled, parts, owner_ref, level_ref, patches_ref, order_ref, wanted_ref, *refs):
+    out_refs, (held, taken, come, gone) = refs[:parts], refs[parts:]
+    owners = held.shape[1]
+    slot_count = order_ref.shape[0]
+    per_owner = slot_count // owners
+
+    def clear(i):
+        taken[i] = 0
+
+    loop(owners, clear)
+    if not filled:
+
+        def empty(i):
+            order_ref[i] = -1
+            wanted_ref[i] = 0
+
+        loop(slot_count, empty)
+
+    def place(i):
+        owner = owner_ref[i]
+        rank = taken[owner]
+        taken[owner] = rank + 1
+        slot = owner * per_owner + rank
+        order_ref[slot] = i
+        wanted_ref[slot] = level_ref[i]
+
+        @pl.when(rank < parts)
+        def _():
+            step = step_of(rank, parts)
+            pltpu.make_async_copy(
+                patches_ref.at[i], held.at[step, owner], come.at[step, owner]
+            ).start()
+
+    loop(owner_ref.shape[0], place)
+    send_on(filled, 0, order_ref, patches_ref, out_refs, held, come, gone)
+
+
+def send_on(filled, chunk, order_ref, patches_ref, out_refs, held, come, gone):
+    parts, owners = held.shape[:2]
+    per_owner = order_ref.shape[0] // owners
+
+    def slot_patch(step, owner):
+        part = lax.rem(lax.axis_index("depth") + step, parts)
+        return order_ref[owner * per_owner + chunk * parts + part]
+
+    for step in [*range(1, parts), 0]:
+
+        def pass_on(owner):
+            def act():
+                pltpu.make_async_copy(
+                    patches_ref.at[0], held.at[step, owner], come.at[step, owner]
+                ).wait()
+
+            guard(filled, slot_patch(step, owner) >= 0, act)
+            pltpu.make_async_copy(
+                held.at[step, owner], out_refs[step].at[owner], gone.at[step, owner]
+            ).start()
+
+        loop(owners, pass_on)
+    for step in range(parts):
+        loop(
+            owners,
+            lambda owner: pltpu.make_async_copy(
+                held.at[step, owner], out_refs[step].at[owner], gone.at[step, owner]
+            ).wait(),
+        )
+
+
+def scratch_of(parts, owners, block):
+    return [
+        pltpu.VMEM((parts, owners) + block, jnp.float32),
+        pltpu.SemaphoreType.DMA((parts, owners)),
+        pltpu.SemaphoreType.DMA((parts, owners)),
+    ]
+
+
+ANYWHERE = pl.BlockSpec(memory_space=pl.ANY)
+SCALARS = pl.BlockSpec(memory_space=pltpu.SMEM)
+
+
+def route(owner, level, patches, owners, parts, slot_count, filled):
+    block = patches.shape[1:]
+    held, come, gone = scratch_of(parts, owners, block)
+    return pl.pallas_call(
+        functools.partial(route_kernel, filled, parts),
+        in_specs=[SCALARS, SCALARS, ANYWHERE],
+        out_specs=[SCALARS, SCALARS] + [ANYWHERE] * parts,
+        out_shape=[jax.ShapeDtypeStruct((slot_count,), jnp.int32)] * 2
+        + [jax.ShapeDtypeStruct((owners,) + block, patches.dtype)] * parts,
+        scratch_shapes=[held, pltpu.SMEM((owners,), jnp.int32), come, gone],
+        name="route",
+    )(owner, level, patches)
+
+
+def chunk_kernel(filled, chunk, order_ref, patches_ref, *refs):
+    out_refs, (held, come, gone) = refs[-3 - refs[-3].shape[0] : -3], refs[-3:]
+    parts, owners = held.shape[:2]
+    per_owner = order_ref.shape[0] // owners
+    for step in range(parts):
+
+        def fetch(owner):
+            part = lax.rem(lax.axis_index("depth") + step, parts)
+            number = order_ref[owner * per_owner + chunk * parts + part]
+
+            def act():
+                pltpu.make_async_copy(
+                    patches_ref.at[number], held.at[step, owner], come.at[step, owner]
+                ).start()
+
+            guard(filled, number >= 0, act)
+
+        loop(owners, fetch)
+    send_on(filled, chunk, order_ref, patches_ref, out_refs, held, come, gone)
+
+
+def fetch_chunk(order, patches, owners, parts, chunk, filled):
+    block = patches.shape[1:]
+    return pl.pallas_call(
+        functools.partial(chunk_kernel, filled, chunk),
+        in_specs=[SCALARS, ANYWHERE],
+        out_specs=[ANYWHERE] * parts,
+        out_shape=[jax.ShapeDtypeStruct((owners,) + block, patches.dtype)] * parts,
+        scratch_shapes=scratch_of(parts, owners, block),
+        name="fetch_chunk",
+    )(order, patches)
+
+
+def store_kernel(filled, chunk, parts, order_ref, *refs):
+    source_refs, out_ref, (held, come, gone) = refs[:parts], refs[-4], refs[-3:]
+    owners = held.shape[1]
+    per_owner = order_ref.shape[0] // owners
+
+    def fetch(step, owner):
+        return pltpu.make_async_copy(
+            source_refs[step].at[owner], held.at[step, owner], come.at[step, owner]
+        )
+
+    def store(step, owner, number):
+        return pltpu.make_async_copy(
+            held.at[step, owner], out_ref.at[number], gone.at[step, owner]
+        )
+
+    def each(act):
+        for step in range(parts):
+
+            def one(owner):
+                part = lax.rem(lax.axis_index("depth") + (parts - step), parts)
+                number = order_ref[owner * per_owner + chunk * parts + part]
+                guard(filled, number >= 0, lambda: act(step, owner, number))
+
+            loop(owners, one)
+
+    def pass_on(step, owner, number):
+        fetch(step, owner).wait()
+        store(step, owner, number).start()
+
+    each(lambda step, owner, number: fetch(step, owner).start())
+    each(pass_on)
+    each(lambda step, owner, number: store(step, owner, number).wait())
+
+
+def store_chunk(order, sources, into, out_shape, chunk, filled):
+    parts, owners, block = len(sources), sources[0].shape[0], sources[0].shape[1:]
+    operands = sources if into is None else sources + [into]
+    return pl.pallas_call(
+        functools.partial(store_kernel, filled, chunk, parts),
+        in_specs=[SCALARS] + [ANYWHERE] * len(operands),
+        out_specs=ANYWHERE,
+        out_shape=jax.ShapeDtypeStruct(out_shape, jnp.float32),
+        scratch_shapes=scratch_of(parts, owners, block),
+        input_output_aliases={} if into is None else {len(operands): 0},
+        name="store_chunk",
+    )(order, *operands)
+
+
+def pick_kernel(parts, chunk, wanted_ref, source_ref, out_ref, held, come, gone):
+    count = held.shape[0]
+    per_source = wanted_ref.shape[0] * parts // count
+
+    def fetch(i):
+        level = wanted_ref[i // parts * per_source + chunk * parts + lax.rem(i, parts)]
+        return pltpu.make_async_copy(source_ref.at[level], held.at[i], come.at[i])
+
+    def store(i):
+        return pltpu.make_async_copy(held.at[i], out_ref.at[i], gone.at[i])
+
+    def pass_on(i):
+        fetch(i).wait()
+        store(i).start()
+
+    loop(count, lambda i: fetch(i).start())
+    loop(count, pass_on)
+    loop(count, lambda i: store(i).wait())
+
+
+def pick_phases(wanted, phases, owners, parts, chunk):
+    count, block = owners * parts, phases.shape[1:]
+    return pl.pallas_call(
+        functools.partial(pick_kernel, parts, chunk),
+        in_specs=[SCALARS, ANYWHERE],
+        out_specs=ANYWHERE,
+        out_shape=jax.ShapeDtypeStruct((count,) + block, phases.dtype),
+        scratch_shapes=[
+            pltpu.VMEM((count,) + block, phases.dtype),
+            pltpu.SemaphoreType.DMA((count,)),
+            pltpu.SemaphoreType.DMA((count,)),
+        ],
+        name="pick_phases",
+    )(wanted, phases)
+
+
+def spread(arrays):
+    parts = len(arrays)
+    return arrays[:1] + [
+        lax.ppermute(arrays[step], "depth", [(i, (i + step) % parts) for i in range(parts)])
+        for step in range(1, parts)
+    ]
+
+
+def exchange(values, axes):
+    return lax.all_to_all(values, axes, split_axis=0, concat_axis=0, tiled=True)
+
+
+def by_chunks(patches, patch_owner, patch_level, phases):
+    patch_count, _, extent = patches.shape
+    owners, parts = lax.axis_size("tile"), lax.axis_size("depth")
     slot_count = owners * CAP
     filled = slot_count == patch_count
-    direct = CAP % parts == 0
+    columns = phases.shape[1]
+    order, wanted, *sent = route(
+        patch_owner[:, 0], patch_level, patches, owners, parts, slot_count, filled
+    )
+    wanted = exchange(wanted.reshape(owners, CAP), "tile").reshape(-1)
+    result = None
+    for chunk in range(CAP // parts):
+        if chunk:
+            sent = fetch_chunk(order, patches, owners, parts, chunk, filled)
+        fields = spread(list(sent))
+        picked = pick_phases(wanted, phases, owners, parts, chunk)
+        phase = exchange(picked, ("tile", "depth"))
+        local = refocus(fields, phase.reshape(owners, parts, columns, extent))
+        backs = spread(list(local))
+        result = store_chunk(order, backs, result, patches.shape, chunk, filled)
+    return result
+
+
+def by_owner(patches, patch_owner, patch_level, phases):
+    patch_count, row_count, extent = patches.shape
+    owners, parts = lax.axis_size("tile"), lax.axis_size("depth")
+    slot_count = owners * CAP
+    filled = slot_count == patch_count
     owner = patch_owner[:, 0]
     numbers = jnp.arange(patch_count, dtype=jnp.int32)
     rank = jnp.sum(
@@ -187,42 +466,25 @@
         axis=1,
         dtype=jnp.int32,
     )
-    slot = owner * CAP + rank
-    slot_hot = jnp.arange(slot_count, dtype=jnp.int32)[:, None] == slot[None, :]
-    level_of_slot = jnp.sum(jnp.where(slot_hot, patch_level[None, :], 0), axis=1, dtype=jnp.int32)
-    patch_of_slot = jnp.sum(jnp.where(slot_hot, numbers[None, :] + 1, 0), axis=1, dtype=jnp.int32) - 1
-    wanted = lax.all_to_all(
-        level_of_slot.reshape(owners, CAP), "tile", split_axis=0, concat_axis=0, tiled=True
-    )
+    slot_hot = jnp.arange(slot_count, dtype=jnp.int32)[:, None] == (owner * CAP + rank)[None, :]
+    wanted = jnp.sum(jnp.where(slot_hot, patch_level[None, :], 0), axis=1, dtype=jnp.int32)
+    order = jnp.sum(jnp.where(slot_hot, numbers[None, :] + 1, 0), axis=1, dtype=jnp.int32) - 1
+    wanted = exchange(wanted.reshape(owners, CAP), "tile").reshape(-1)
+    field = exchange(move(order, patches, (slot_count,) + patches.shape[1:], False, filled), "depth")
+    picked = move(wanted, phases, (slot_count,) + phases.shape[1:], False, True)
+    phase = exchange(exchange(picked, "tile"), "depth")
+    (local,) = refocus(
+        [field.reshape(parts, -1, row_count, extent)],
+        phase.reshape((parts, -1) + phases.shape[1:]),
+    )
+    back = exchange(local.reshape(-1, row_count, extent), "depth")
+    return move(order, back, patches.shape, True, filled)
+
+
+def on_device(patches, patch_owner, patch_level, phases):
     turned = jnp.transpose(phases, (0, 2, 1))
-    columns = turned.shape[1]
-    chunks = CAP // parts if direct else 1
-    result = None
-    for chunk in range(chunks):
-        if direct:
-            order = patch_of_slot.reshape(owners, parts, chunks)[:, :, chunk].T.reshape(-1)
-            levels = wanted.reshape(owners, parts, chunks)[:, :, chunk].reshape(-1)
-        else:
-            order, levels = patch_of_slot, wanted.reshape(-1)
-        sent = gather(order, patches, filled)
-        field = lax.all_to_all(sent, "depth", split_axis=0, concat_axis=0, tiled=True)
-        field = field.reshape(parts, -1, row_count, extent)
-        picked = gather(levels, turned, True)
-        if direct:
-            phase = lax.all_to_all(
-                picked, ("tile", "depth"), split_axis=0, concat_axis=0, tiled=True
-            ).reshape(owners, parts, columns, extent)
-        else:
-            picked = lax.all_to_all(picked, "tile", split_axis=0, concat_axis=0, tiled=True)
-            phase = lax.all_to_all(
-                picked, "depth", split_axis=0, concat_axis=0, tiled=True
-            ).reshape(parts, -1, columns, extent)
-        local = refocus(field, phase, direct)
-        back = lax.all_to_all(
-            local.reshape(-1, row_count, extent), "depth", split_axis=0, concat_axis=0, tiled=True
-        )
-        result = move(order, back, patches.shape, True, filled, result)
-    return result
+    plan = by_chunks if CAP % lax.axis_size("depth") == 0 else by_owner
+    return plan(patches, patch_owner, patch_level, turned)
 
 
 def solution(mesh):

time: 335 us -> 335 us (level)
  the two profiles are of different devices: /device:TPU:0 before, /device:TPU:8 now
where the time goes in v3:
time: 335 us; the launch traced here: 334 us
  waiting for transfers between devices  218 us (65%)
  Pallas kernels  77.4 us (23%)
  starting transfers between devices  22.9 us (7%)
  blocking collectives  8.12 us (2%)
  local copies, waits for them, and re-layouts  6.44 us (2%)
    ppermute x12, waiting for transfers between devices, spread(): lax.ppermute(arrays[step], 'depth', [(i, (i + step) % parts) for i in ran...  173 us
    pallas_call x2, Pallas kernels, refocus(): pl.pallas_call(functools.partial(refocus_kernel, pieces), grid=(slots,),...  54.4 us
    all_to_all x2, waiting for transfers between devices, exchange(): return lax.all_to_all(values, axes, split_axis=0, concat_axis=0, tiled=True)  45.2 us
    ppermute x12, starting transfers between devices, spread(): lax.ppermute(arrays[step], 'depth', [(i, (i + step) % parts) for i in ran...  16.2 us
    all_to_all x1, blocking collectives, exchange(): return lax.all_to_all(values, axes, split_axis=0, concat_axis=0, tiled=True)  8.12 us
    pallas_call x2, Pallas kernels, pick_phases(): pl.pallas_call(functools.partial(pick_kernel, parts, chunk), in_specs=[SC...  7.03 us
    pallas_call x2, Pallas kernels, store_chunk(): pl.pallas_call(functools.partial(store_kernel, filled, chunk, parts), in_...  6.92 us
  transfers between devices with their start and end apart: 14, of which 7 were waited for; matrix products, arithmetic and copies ran while one was open for 0% of the time, Pallas kernels for 20%

profile of v3, /device:TPU:8, one launch (start us, length us, event | category | flops | bytes accessed | tf_op | source)
XLA Modules:
  0.0 333.9 jit_solution(14670161890109218941)
XLA Ops:
  0.0 5.2 %route.1 = (s32[64]{0:T(128)}, s32[64]{0:T(128)}, f32[8,64,256]{2,1,0:T(8,128)}, f32[8,64,256]{2,1,0:T(8,128)}, f32[8,64,256]{2,1,0:T(8,128)}, /*index=5*/f32[8,64,256]{2,1,0:T(8,128)}) custom-call(s32[64]{0:T(128)} %bitcast.10, s32[64]{0:T(128)} %level_ref.1, f32[64,64,256]{2,1,0:T(8,128)} %patches_ref.3), custom_call_target="tpu_custom_call" | custom-call | tf_op jit(solution)/shard_map/route/pallas_call | solution.py:294
  5.2 0.7 all_to_all.12
  5.9 8.1 %all_to_all.19 = s32[8,1,8]{2,1,0:T(1,128)S(1)} all-to-all(s32[8,1,8]{2,1,0:T(1,128)S(1)} %bitcast.9), channel_id=1, replica_groups=mesh['tile'=8,'depth'=4] {'tile'}, dimensions={0} | all-to-all | bytes 512 | tf_op jit(solution)/shard_map/all_to_all | solution.py:431
  14.0 0.5 broadcast.3
  14.5 0.7 reduce.3
  15.2 0.6 reshape.14.wanted_ref
  15.8 3.5 %pick_phases.3 = f32[32,64,256]{2,1,0:T(8,128)} custom-call(s32[64]{0:T(128)} %reshape.14.wanted_ref, f32[64,64,256]{2,1,0:T(8,128)} %bitcast.5), custom_call_target="tpu_custom_call" | custom-call | tf_op jit(solution)/shard_map/pick_phases/pallas_call | solution.py:408
  19.4 4.0 %all-to-all-start.2 = ((f32[32,64,256]{2,1,0:T(8,128)}), f32[32,64,256]{2,1,0:T(8,128)S(1)}, u32[]{:S(2)}, u32[]{:S(2)}) async-start(f32[32,64,256]{2,1,0:T(8,128)} %pick_phases.3), calls=%async_computation.2 | async-start | bytes 4194304 | tf_op jit(solution)/shard_map/all_to_all | solution.py:431
  23.3 3.5 %pick_phases.2 = f32[32,64,256]{2,1,0:T(8,128)} custom-call(s32[64]{0:T(128)} %reshape.14.wanted_ref, f32[64,64,256]{2,1,0:T(8,128)} %bitcast.6), custom_call_target="tpu_custom_call" | custom-call | tf_op jit(solution)/shard_map/pick_phases/pallas_call | solution.py:408
  26.8 45.2 %all-to-all-done.2 = f32[32,64,256]{2,1,0:T(8,128)S(1)} async-done(((f32[32,64,256]{2,1,0:T(8,128)}), f32[32,64,256]{2,1,0:T(8,128)S(1)}, u32[]{:S(2)}, u32[]{:S(2)}) %all-to-all-start.2) | async-done | bytes 2097184 | tf_op jit(solution)/shard_map/all_to_all | solution.py:431
  72.1 1.3 copy-done.1
  73.4 2.7 all-to-all-start.1
  76.1 1.5 collective-permute-start.6
  77.7 1.1 collective-permute-start.7
  78.8 1.8 collective-permute-start.8
  80.6 3.8 %fetch_chunk.1 = (f32[8,64,256]{2,1,0:T(8,128)}, f32[8,64,256]{2,1,0:T(8,128)}, f32[8,64,256]{2,1,0:T(8,128)}, f32[8,64,256]{2,1,0:T(8,128)}) custom-call(s32[64]{0:T(128)} %get-tuple-element.23.order_ref, f32[64,64,256]{2,1,0:T(8,128)} %patches_ref.3), custom_call_target="tpu_custom_call" | custom-call | tf_op jit(solution)/shard_map/fetch_chunk/pallas_call | solution.py:328
  84.5 0.3 collective-permute-start
  84.7 3.6 %collective-permute-start.1 = (f32[8,64,256]{2,1,0:T(8,128)}, f32[8,64,256]{2,1,0:T(8,128)}, u32[]{:S(2)}, u32[]{:S(2)}) collective-permute-start(f32[8,64,256]{2,1,0:T(8,128)} %get-tuple-element.26), channel_id=1, source_target_pairs={{0,2},{1,3},{2,0},{3,1},{4,6},{5,7},{6,4},{7,5},{8,10},{9,11},{10,... | collective-permute-start | bytes 1572872 | tf_op jit(solution)/shard_map/ppermute | solution.py:425
  88.3 67.9 %collective-permute-done.6.refs_1_ = f32[8,64,256]{2,1,0:T(8,128)S(1)} collective-permute-done((f32[8,64,256]{2,1,0:T(8,128)}, f32[8,64,256]{2,1,0:T(8,128)S(1)}, u32[]{:S(2)}, u32[]{:S(2)}) %collective-permute-start.6) | collective-permute-done | bytes 524320 | tf_op jit(solution)/shard_map/ppermute | solution.py:425
  156.2 0.0 collective-permute-start.2
  156.2 33.6 %collective-permute-done.7.refs_2_ = f32[8,64,256]{2,1,0:T(8,128)} collective-permute-done((f32[8,64,256]{2,1,0:T(8,128)}, f32[8,64,256]{2,1,0:T(8,128)}, u32[]{:S(2)}, u32[]{:S(2)}) %collective-permute-start.7) | collective-permute-done | bytes 524320 | tf_op jit(solution)/shard_map/ppermute | solution.py:425
  189.8 2.2 collective-permute-done.8.refs_3_
  191.9 27.2 %refocus.3 = (f32[8,64,256]{2,1,0:T(8,128)}, f32[8,64,256]{2,1,0:T(8,128)}, f32[8,64,256]{2,1,0:T(8,128)}, f32[8,64,256]{2,1,0:T(8,128)}) custom-call(bf16[4,256,256]{2,1,0:T(8,128)(2,1)} %constant.2.clone.table_ref, f32[8,64,256]{2,1,0:T(8,128)} %get-tuple-element.33.refs_0_, f32[8,64,256]{2,1,0:T(8,128)} %copy-done.4, ...), custom_call_target="tpu_custom_call" | custom-call | tf_op jit(solution)/shard_map/refocus/pallas_call | solution.py:122
  219.2 0.0 collective-permute-start.9
  219.2 0.0 collective-permute-done.refs_1_
  219.2 0.0 collective-permute-done.1.refs_2_
  219.2 0.0 collective-permute-done.2.refs_3_
  219.2 0.0 all-to-all-done.1
  219.3 0.0 copy-start
  219.3 0.7 copy-done.3
  220.0 0.7 copy-done
  220.7 27.2 %refocus.2 = (f32[8,64,256]{2,1,0:T(8,128)}, f32[8,64,256]{2,1,0:T(8,128)}, f32[8,64,256]{2,1,0:T(8,128)}, f32[8,64,256]{2,1,0:T(8,128)}) custom-call(bf16[4,256,256]{2,1,0:T(8,128)(2,1)} %constant.2.clone.table_ref, f32[8,64,256]{2,1,0:T(8,128)} %get-tuple-element.24.refs_0_, f32[8,64,256]{2,1,0:T(8,128)} %copy-done.3, ...), custom_call_target="tpu_custom_call" | custom-call | tf_op jit(solution)/shard_map/refocus/pallas_call | solution.py:122
  247.9 1.8 collective-permute-start.3
  249.7 2.6 collective-permute-start.10
  252.3 0.0 collective-permute-start.11
  252.3 0.6 collective-permute-start.4
  252.9 0.0 collective-permute-done.9.refs_1_
  252.9 2.8 collective-permute-start.5
  255.8 62.7 %collective-permute-done.10.refs_2_ = f32[8,64,256]{2,1,0:T(8,128)S(1)} collective-permute-done((f32[8,64,256]{2,1,0:T(8,128)}, f32[8,64,256]{2,1,0:T(8,128)S(1)}, u32[]{:S(2)}, u32[]{:S(2)}) %collective-permute-start.10) | collective-permute-done | bytes 524320 | tf_op jit(solution)/shard_map/ppermute | solution.py:425
  318.5 0.0 collective-permute-done.11.refs_3_
  318.5 0.8 copy-done.5
  319.3 0.2 copy-done.6
  319.5 3.5 %store_chunk.2.refs_4_ = f32[64,64,256]{2,1,0:T(8,128)} custom-call(s32[64]{0:T(128)} %get-tuple-element.23.order_ref, f32[8,64,256]{2,1,0:T(8,128)} %get-tuple-element.37.refs_0_, f32[8,64,256]{2,1,0:T(8,128)} %copy-done.2, f32[8,64,256]{2,1,0:T(8,128)} %copy-done.5, f32[8,64,256]{2,1,0:T(8,128)} %copy-done.6), custom_call_target="tpu_custom_call" | custom-call | tf_op jit(solution)/shard_map/store_chunk/pallas_call | solution.py:375
  322.9 0.0 collective-permute-done.3.refs_1_
  323.0 4.5 %collective-permute-done.4.refs_2_ = f32[8,64,256]{2,1,0:T(8,128)S(1)} collective-permute-done((f32[8,64,256]{2,1,0:T(8,128)}, f32[8,64,256]{2,1,0:T(8,128)S(1)}, u32[]{:S(2)}, u32[]{:S(2)}) %collective-permute-start.4) | collective-permute-done | bytes 524320 | tf_op jit(solution)/shard_map/ppermute | solution.py:425
  327.4 2.2 collective-permute-done.5.refs_3_
  329.7 0.8 copy-done.9
  330.5 3.5 %store_chunk.3 = f32[64,64,256]{2,1,0:T(8,128)} custom-call(s32[64]{0:T(128)} %get-tuple-element.23.order_ref, f32[8,64,256]{2,1,0:T(8,128)} %get-tuple-element.29.refs_0_, f32[8,64,256]{2,1,0:T(8,128)} %copy-done.7, f32[8,64,256]{2,1,0:T(8,128)} %copy-done.8, f32[8,64,256]{2,1,0:T(8,128)} %copy-done.9, ...), custom_call_target="tpu_custom_call", output_to_operand_aliasing={{}: (5, {})} | custom-call | tf_op jit(solution)/shard_map/store_chunk/pallas_call | solution.py:375
  (13 shorter events, 0.0 us)
Async XLA Ops:
  19.4 52.7 %all-to-all-start.2 = ((f32[32,64,256]{2,1,0:T(8,128)}), f32[32,64,256]{2,1,0:T(8,128)S(1)}, u32[]{:S(2)}, u32[]{:S(2)}) async-start(f32[32,64,256]{2,1,0:T(8,128)} %pick_phases.3), calls=%async_computation.2 | async-start | bytes 4194304 | tf_op jit(solution)/shard_map/all_to_all | solution.py:431
  72.1 1.3 copy-start.1
  73.4 145.8 %all-to-all-start.1 = ((f32[32,64,256]{2,1,0:T(8,128)}), f32[32,64,256]{2,1,0:T(8,128)S(1)}, u32[]{:S(2)}, u32[]{:S(2)}) async-start(f32[32,64,256]{2,1,0:T(8,128)} %pick_phases.2), calls=%async_computation.1 | async-start | bytes 4194304 | tf_op jit(solution)/shard_map/all_to_all | solution.py:431
  76.1 80.1 %collective-permute-start.6 = (f32[8,64,256]{2,1,0:T(8,128)}, f32[8,64,256]{2,1,0:T(8,128)S(1)}, u32[]{:S(2)}, u32[]{:S(2)}) collective-permute-start(f32[8,64,256]{2,1,0:T(8,128)} %get-tuple-element.34), channel_id=1, source_target_pairs={{0,1},{1,2},{2,3},{3,0},{4,5},{5,6},{6,7},{7,4},{8,9},{9,10},{10,1... | collective-permute-start | bytes 1572872 | tf_op jit(solution)/shard_map/ppermute | solution.py:425
  77.7 112.1 %collective-permute-start.7 = (f32[8,64,256]{2,1,0:T(8,128)}, f32[8,64,256]{2,1,0:T(8,128)}, u32[]{:S(2)}, u32[]{:S(2)}) collective-permute-start(f32[8,64,256]{2,1,0:T(8,128)} %get-tuple-element.35), channel_id=1, source_target_pairs={{0,2},{1,3},{2,0},{3,1},{4,6},{5,7},{6,4},{7,5},{8,10},{9,11},{10,... | collective-permute-start | bytes 1572872 | tf_op jit(solution)/shard_map/ppermute | solution.py:425
  78.8 113.1 %collective-permute-start.8 = (f32[8,64,256]{2,1,0:T(8,128)}, f32[8,64,256]{2,1,0:T(8,128)}, u32[]{:S(2)}, u32[]{:S(2)}) collective-permute-start(f32[8,64,256]{2,1,0:T(8,128)} %get-tuple-element.36), channel_id=1, source_target_pairs={{0,3},{1,0},{2,1},{3,2},{4,7},{5,4},{6,5},{7,6},{8,11},{9,8},{10,9... | collective-permute-start | bytes 1572872 | tf_op jit(solution)/shard_map/ppermute | solution.py:425
  84.5 134.7 %collective-permute-start = (f32[8,64,256]{2,1,0:T(8,128)}, f32[8,64,256]{2,1,0:T(8,128)S(1)}, u32[]{:S(2)}, u32[]{:S(2)}) collective-permute-start(f32[8,64,256]{2,1,0:T(8,128)} %get-tuple-element.25), channel_id=1, source_target_pairs={{0,1},{1,2},{2,3},{3,0},{4,5},{5,6},{6,7},{7,4},{8,9},{9,10},{10,1... | collective-permute-start | bytes 1572872 | tf_op jit(solution)/shard_map/ppermute | solution.py:425
  84.7 134.5 %collective-permute-start.1 = (f32[8,64,256]{2,1,0:T(8,128)}, f32[8,64,256]{2,1,0:T(8,128)}, u32[]{:S(2)}, u32[]{:S(2)}) collective-permute-start(f32[8,64,256]{2,1,0:T(8,128)} %get-tuple-element.26), channel_id=1, source_target_pairs={{0,2},{1,3},{2,0},{3,1},{4,6},{5,7},{6,4},{7,5},{8,10},{9,11},{10,... | collective-permute-start | bytes 1572872 | tf_op jit(solution)/shard_map/ppermute | solution.py:425
  156.2 35.7 %copy-start.4 = (f32[8,64,256]{2,1,0:T(8,128)}, f32[8,64,256]{2,1,0:T(8,128)S(1)}, u32[]{:S(2)}) copy-start(f32[8,64,256]{2,1,0:T(8,128)S(1)} %collective-permute-done.6.refs_1_) | copy-start | bytes 1572868
  156.2 63.0 %collective-permute-start.2 = (f32[8,64,256]{2,1,0:T(8,128)}, f32[8,64,256]{2,1,0:T(8,128)}, u32[]{:S(2)}, u32[]{:S(2)}) collective-permute-start(f32[8,64,256]{2,1,0:T(8,128)} %get-tuple-element.27), channel_id=1, source_target_pairs={{0,3},{1,0},{2,1},{3,2},{4,7},{5,4},{6,5},{7,6},{8,11},{9,8},{10,9... | collective-permute-start | bytes 1572872 | tf_op jit(solution)/shard_map/ppermute | solution.py:425
  219.2 33.8 %collective-permute-start.9 = (f32[8,64,256]{2,1,0:T(8,128)}, f32[8,64,256]{2,1,0:T(8,128)S(1)}, u32[]{:S(2)}, u32[]{:S(2)}) collective-permute-start(f32[8,64,256]{2,1,0:T(8,128)} %get-tuple-element.38), channel_id=1, source_target_pairs={{0,1},{1,2},{2,3},{3,0},{4,5},{5,6},{6,7},{7,4},{8,9},{9,10},{10,1... | collective-permute-start | bytes 1572872 | tf_op jit(solution)/shard_map/ppermute | solution.py:425
  219.2 0.8 copy-start.3
  219.3 1.4 copy-start
  247.9 75.0 %collective-permute-start.3 = (f32[8,64,256]{2,1,0:T(8,128)}, f32[8,64,256]{2,1,0:T(8,128)S(1)}, u32[]{:S(2)}, u32[]{:S(2)}) collective-permute-start(f32[8,64,256]{2,1,0:T(8,128)} %get-tuple-element.30), channel_id=1, source_target_pairs={{0,1},{1,2},{2,3},{3,0},{4,5},{5,6},{6,7},{7,4},{8,9},{9,10},{10,1... | collective-permute-start | bytes 1572872 | tf_op jit(solution)/shard_map/ppermute | solution.py:425
  249.7 68.8 %collective-permute-start.10 = (f32[8,64,256]{2,1,0:T(8,128)}, f32[8,64,256]{2,1,0:T(8,128)S(1)}, u32[]{:S(2)}, u32[]{:S(2)}) collective-permute-start(f32[8,64,256]{2,1,0:T(8,128)} %get-tuple-element.39), channel_id=1, source_target_pairs={{0,2},{1,3},{2,0},{3,1},{4,6},{5,7},{6,4},{7,5},{8,10},{9,11},{10,... | collective-permute-start | bytes 1572872 | tf_op jit(solution)/shard_map/ppermute | solution.py:425
  252.3 66.2 %collective-permute-start.11 = (f32[8,64,256]{2,1,0:T(8,128)}, f32[8,64,256]{2,1,0:T(8,128)S(1)}, u32[]{:S(2)}, u32[]{:S(2)}) collective-permute-start(f32[8,64,256]{2,1,0:T(8,128)} %get-tuple-element.40), channel_id=1, source_target_pairs={{0,3},{1,0},{2,1},{3,2},{4,7},{5,4},{6,5},{7,6},{8,11},{9,8},{10,9... | collective-permute-start | bytes 1572872 | tf_op jit(solution)/shard_map/ppermute | solution.py:425
  252.3 75.2 %collective-permute-start.4 = (f32[8,64,256]{2,1,0:T(8,128)}, f32[8,64,256]{2,1,0:T(8,128)S(1)}, u32[]{:S(2)}, u32[]{:S(2)}) collective-permute-start(f32[8,64,256]{2,1,0:T(8,128)} %get-tuple-element.31), channel_id=1, source_target_pairs={{0,2},{1,3},{2,0},{3,1},{4,6},{5,7},{6,4},{7,5},{8,10},{9,11},{10,... | collective-permute-start | bytes 1572872 | tf_op jit(solution)/shard_map/ppermute | solution.py:425
  252.9 65.6 %copy-start.2 = (f32[8,64,256]{2,1,0:T(8,128)}, f32[8,64,256]{2,1,0:T(8,128)S(1)}, u32[]{:S(2)}) copy-start(f32[8,64,256]{2,1,0:T(8,128)S(1)} %collective-permute-done.9.refs_1_) | copy-start | bytes 1572868
  252.9 76.7 %collective-permute-start.5 = (f32[8,64,256]{2,1,0:T(8,128)}, f32[8,64,256]{2,1,0:T(8,128)S(1)}, u32[]{:S(2)}, u32[]{:S(2)}) collective-permute-start(f32[8,64,256]{2,1,0:T(8,128)} %get-tuple-element.32), channel_id=1, source_target_pairs={{0,3},{1,0},{2,1},{3,2},{4,7},{5,4},{6,5},{7,6},{8,11},{9,8},{10,9... | collective-permute-start | bytes 1572872 | tf_op jit(solution)/shard_map/ppermute | solution.py:425
  318.5 0.8 copy-start.5
  318.5 1.0 copy-start.6
  323.0 6.7 %copy-start.7 = (f32[8,64,256]{2,1,0:T(8,128)}, f32[8,64,256]{2,1,0:T(8,128)S(1)}, u32[]{:S(2)}) copy-start(f32[8,64,256]{2,1,0:T(8,128)S(1)} %collective-permute-done.3.refs_1_) | copy-start | bytes 1572868
  327.4 2.2 copy-start.8
  329.7 0.8 copy-start.9

commit v4 on v3

--- a/solution.py
+++ b/solution.py
@@ -55,9 +55,12 @@
 NT = ((1,), (1,))
 
 
-def rotated(step, parts, rows):
-    part = lax.rem(lax.axis_index("depth") + (step + parts), parts)
-    return pl.ds(pl.multiple_of(part * rows, rows), rows)
+def partner(step):
+    return lax.bitwise_xor(lax.axis_index("depth"), step)
+
+
+def rows_with(step, rows):
+    return pl.ds(pl.multiple_of(partner(step) * rows, rows), rows)
 
 
 def refocus_kernel(pieces, table_ref, *refs):
@@ -84,7 +87,7 @@
         patch = field_refs[0][...].reshape(extent, extent)
     else:
         for step, ref in enumerate(field_refs):
-            whole_ref[rotated(-step, pieces, ref.shape[1]), :] = ref[0]
+            whole_ref[rows_with(step, ref.shape[1]), :] = ref[0]
         patch = whole_ref[...]
     half_turned = product(
         (left_ref[0, :, :extent], left_ref[1, :, :extent]), split(patch), NT
@@ -106,11 +109,13 @@
     else:
         whole_ref[...] = intensity
         for step, ref in enumerate(out_refs):
-            ref[0] = whole_ref[rotated(step, pieces, ref.shape[1]), :]
+            ref[0] = whole_ref[rows_with(step, ref.shape[1]), :]
 
 
 def refocus(fields, phase):
     pieces, extent = len(fields), phase.shape[-1]
+    fields = [pltpu.with_memory_space_constraint(field, pltpu.HBM) for field in fields]
+    phase = pltpu.with_memory_space_constraint(phase, pltpu.HBM)
     if pieces == 1:
         parts, slots, rows, _ = fields[0].shape
         field_spec = pl.BlockSpec((parts, 1, rows, extent), lambda i: (0, i, 0, 0))
@@ -204,13 +209,9 @@
         pl.when(condition)(act)
 
 
-def step_of(part, parts):
-    return lax.rem(part - lax.axis_index("depth") + parts, parts)
-
-
 def route_kernel(filled, parts, owner_ref, level_ref, patches_ref, order_ref, wanted_ref, *refs):
-    out_refs, (held, taken, come, gone) = refs[:parts], refs[parts:]
-    owners = held.shape[1]
+    out_refs, (taken, come) = refs[:parts], refs[parts:]
+    owners = out_refs[0].shape[0]
     slot_count = order_ref.shape[0]
     per_owner = slot_count // owners
 
@@ -233,16 +234,27 @@
         slot = owner * per_owner + rank
         order_ref[slot] = i
         wanted_ref[slot] = level_ref[i]
-
-        @pl.when(rank < parts)
-        def _():
-            step = step_of(rank, parts)
-            pltpu.make_async_copy(
-                patches_ref.at[i], held.at[step, owner], come.at[step, owner]
-            ).start()
+        step = partner(rank)
+        for at in range(parts):
+
+            @pl.when((rank < parts) & (step == at))
+            def _():
+                pltpu.make_async_copy(
+                    patches_ref.at[i], out_refs[at].at[owner], come.at[at, owner]
+                ).start()
 
     loop(owner_ref.shape[0], place)
-    send_on(filled, 0, order_ref, patches_ref, out_refs, held, come, gone)
+    for step in range(parts):
+
+        def arrive(owner):
+            def act():
+                pltpu.make_async_copy(
+                    patches_ref.at[0], out_refs[step].at[owner], come.at[step, owner]
+                ).wait()
+
+            guard(filled, order_ref[owner * per_owner + partner(step)] >= 0, act)
+
+        loop(owners, arrive)
 
 
 def send_on(filled, chunk, order_ref, patches_ref, out_refs, held, come, gone):
@@ -250,8 +262,7 @@
     per_owner = order_ref.shape[0] // owners
 
     def slot_patch(step, owner):
-        part = lax.rem(lax.axis_index("depth") + step, parts)
-        return order_ref[owner * per_owner + chunk * parts + part]
+        return order_ref[owner * per_owner + chunk * parts + partner(step)]
 
     for step in [*range(1, parts), 0]:
 
@@ -290,14 +301,16 @@
 
 def route(owner, level, patches, owners, parts, slot_count, filled):
     block = patches.shape[1:]
-    held, come, gone = scratch_of(parts, owners, block)
     return pl.pallas_call(
         functools.partial(route_kernel, filled, parts),
         in_specs=[SCALARS, SCALARS, ANYWHERE],
-        out_specs=[SCALARS, SCALARS] + [ANYWHERE] * parts,
+        out_specs=[SCALARS, SCALARS] + [pl.BlockSpec(memory_space=pltpu.VMEM)] * parts,
         out_shape=[jax.ShapeDtypeStruct((slot_count,), jnp.int32)] * 2
         + [jax.ShapeDtypeStruct((owners,) + block, patches.dtype)] * parts,
-        scratch_shapes=[held, pltpu.SMEM((owners,), jnp.int32), come, gone],
+        scratch_shapes=[
+            pltpu.SMEM((owners,), jnp.int32),
+            pltpu.SemaphoreType.DMA((parts, owners)),
+        ],
         name="route",
     )(owner, level, patches)
 
@@ -309,8 +322,7 @@
     for step in range(parts):
 
         def fetch(owner):
-            part = lax.rem(lax.axis_index("depth") + step, parts)
-            number = order_ref[owner * per_owner + chunk * parts + part]
+            number = order_ref[owner * per_owner + chunk * parts + partner(step)]
 
             def act():
                 pltpu.make_async_copy(
@@ -335,49 +347,39 @@
     )(order, patches)
 
 
-def store_kernel(filled, chunk, parts, order_ref, *refs):
-    source_refs, out_ref, (held, come, gone) = refs[:parts], refs[-4], refs[-3:]
-    owners = held.shape[1]
+def store_kernel(filled, chunk, parts, steps, order_ref, *refs):
+    source_refs, out_ref, gone = refs[: len(steps)], refs[-2], refs[-1]
+    owners = gone.shape[1]
     per_owner = order_ref.shape[0] // owners
 
-    def fetch(step, owner):
-        return pltpu.make_async_copy(
-            source_refs[step].at[owner], held.at[step, owner], come.at[step, owner]
-        )
-
-    def store(step, owner, number):
-        return pltpu.make_async_copy(
-            held.at[step, owner], out_ref.at[number], gone.at[step, owner]
-        )
-
     def each(act):
-        for step in range(parts):
+        for at, step in enumerate(steps):
 
             def one(owner):
-                part = lax.rem(lax.axis_index("depth") + (parts - step), parts)
-                number = order_ref[owner * per_owner + chunk * parts + part]
-                guard(filled, number >= 0, lambda: act(step, owner, number))
+                number = order_ref[owner * per_owner + chunk * parts + partner(step)]
+                copy = pltpu.make_async_copy(
+                    source_refs[at].at[owner], out_ref.at[number], gone.at[at, owner]
+                )
+                guard(filled, number >= 0, lambda: act(copy))
 
             loop(owners, one)
 
-    def pass_on(step, owner, number):
-        fetch(step, owner).wait()
-        store(step, owner, number).start()
-
-    each(lambda step, owner, number: fetch(step, owner).start())
-    each(pass_on)
-    each(lambda step, owner, number: store(step, owner, number).wait())
-
-
-def store_chunk(order, sources, into, out_shape, chunk, filled):
-    parts, owners, block = len(sources), sources[0].shape[0], sources[0].shape[1:]
+    each(lambda copy: copy.start())
+    each(lambda copy: copy.wait())
+
+
+def store_chunk(order, sources, into, out_shape, chunk, parts, steps, filled):
+    owners = sources[0].shape[0]
+    sources = [pltpu.with_memory_space_constraint(source, pltpu.VMEM) for source in sources]
     operands = sources if into is None else sources + [into]
     return pl.pallas_call(
-        functools.partial(store_kernel, filled, chunk, parts),
-        in_specs=[SCALARS] + [ANYWHERE] * len(operands),
+        functools.partial(store_kernel, filled, chunk, parts, steps),
+        in_specs=[SCALARS]
+        + [pl.BlockSpec(memory_space=pltpu.VMEM)] * len(sources)
+        + [ANYWHERE] * (into is not None),
         out_specs=ANYWHERE,
         out_shape=jax.ShapeDtypeStruct(out_shape, jnp.float32),
-        scratch_shapes=scratch_of(parts, owners, block),
+        scratch_shapes=[pltpu.SemaphoreType.DMA((len(steps), owners))],
         input_output_aliases={} if into is None else {len(operands): 0},
         name="store_chunk",
     )(order, *operands)
@@ -419,12 +421,14 @@
     )(wanted, phases)
 
 
-def spread(arrays):
+def swap(arrays):
     parts = len(arrays)
-    return arrays[:1] + [
-        lax.ppermute(arrays[step], "depth", [(i, (i + step) % parts) for i in range(parts)])
-        for step in range(1, parts)
-    ]
+    swapped = list(arrays)
+    for step in range(parts - 1, 0, -1):
+        swapped[step] = lax.ppermute(
+            arrays[step], "depth", [(part, part ^ step) for part in range(parts)]
+        )
+    return swapped
 
 
 def exchange(values, axes):
@@ -445,12 +449,26 @@
     for chunk in range(CAP // parts):
         if chunk:
             sent = fetch_chunk(order, patches, owners, parts, chunk, filled)
-        fields = spread(list(sent))
+        fields = swap(sent)
         picked = pick_phases(wanted, phases, owners, parts, chunk)
         phase = exchange(picked, ("tile", "depth"))
         local = refocus(fields, phase.reshape(owners, parts, columns, extent))
-        backs = spread(list(local))
-        result = store_chunk(order, backs, result, patches.shape, chunk, filled)
+        backs = swap(local)
+        last = chunk == CAP // parts - 1
+        every = tuple(range(parts))
+        for steps in (every[:1], every[1:2], every[2:]) if last else (every,):
+            if not steps:
+                continue
+            result = store_chunk(
+                order,
+                [backs[step] for step in steps],
+                result,
+                patches.shape,
+                chunk,
+                parts,
+                steps,
+                filled,
+            )
     return result
 
 

time: 335 us -> 313 us (0.934)
  the two profiles are of different devices: /device:TPU:8 before, /device:TPU:12 now
where the time goes in v4:
time: 313 us; the launch traced here: 312 us
  waiting for transfers between devices  199 us (64%)
  Pallas kernels  77.5 us (25%)
  starting transfers between devices  25.5 us (8%)
  blocking collectives  7.19 us (2%)
    ppermute x12, waiting for transfers between devices, swap(): lax.ppermute(arrays[step], 'depth', [(part, part ^ step) for part in rang...  155 us
    pallas_call x2, Pallas kernels, refocus(): pl.pallas_call(functools.partial(refocus_kernel, pieces), grid=(slots,),...  54.2 us
    all_to_all x2, waiting for transfers between devices, exchange(): return lax.all_to_all(values, axes, split_axis=0, concat_axis=0, tiled=True)  43.9 us
    ppermute x12, starting transfers between devices, swap(): lax.ppermute(arrays[step], 'depth', [(part, part ^ step) for part in rang...  16.6 us
    all_to_all x2, starting transfers between devices, exchange(): return lax.all_to_all(values, axes, split_axis=0, concat_axis=0, tiled=True)  8.91 us
    pallas_call x4, Pallas kernels, store_chunk(): pl.pallas_call(functools.partial(store_kernel, filled, chunk, parts, step...  7.83 us
    pallas_call x2, Pallas kernels, pick_phases(): pl.pallas_call(functools.partial(pick_kernel, parts, chunk), in_specs=[SC...  7.42 us
    all_to_all x1, blocking collectives, exchange(): return lax.all_to_all(values, axes, split_axis=0, concat_axis=0, tiled=True)  7.19 us
  transfers between devices with their start and end apart: 14, of which 8 were waited for; matrix products, arithmetic and copies ran while one was open for 0% of the time, Pallas kernels for 22%

profile of v4, /device:TPU:12, one launch (start us, length us, event | category | flops | bytes accessed | tf_op | source)
XLA Modules:
  0.0 312.3 jit_solution(14814731794329099585)
XLA Ops:
  0.0 4.2 %route.1 = (s32[64]{0:T(128)}, s32[64]{0:T(128)}, f32[8,64,256]{2,1,0:T(8,128)}, f32[8,64,256]{2,1,0:T(8,128)}, f32[8,64,256]{2,1,0:T(8,128)}, /*index=5*/f32[8,64,256]{2,1,0:T(8,128)}) custom-call(s32[64]{0:T(128)} %bitcast.9, s32[64]{0:T(128)} %level_ref.1, f32[64,64,256]{2,1,0:T(8,128)} %patches_ref.3), custom_call_target="tpu_custom_call" | custom-call | tf_op jit(solution)/shard_map/route/pallas_call | solution.py:304
  4.2 0.7 all_to_all.12
  5.0 7.2 %all_to_all.19 = s32[8,1,8]{2,1,0:T(1,128)S(1)} all-to-all(s32[8,1,8]{2,1,0:T(1,128)S(1)} %bitcast.8), channel_id=1, replica_groups=mesh['tile'=8,'depth'=4] {'tile'}, dimensions={0} | all-to-all | bytes 512 | tf_op jit(solution)/shard_map/all_to_all | solution.py:435
  12.1 0.5 broadcast.3
  12.7 0.7 reduce.3
  13.3 0.6 reshape.14.wanted_ref
  13.9 3.5 %pick_phases.3 = f32[32,64,256]{2,1,0:T(8,128)} custom-call(s32[64]{0:T(128)} %reshape.14.wanted_ref, f32[64,64,256]{2,1,0:T(8,128)} %bitcast.5), custom_call_target="tpu_custom_call" | custom-call | tf_op jit(solution)/shard_map/pick_phases/pallas_call | solution.py:410
  17.5 5.2 %all-to-all-start.2 = ((f32[32,64,256]{2,1,0:T(8,128)}), f32[32,64,256]{2,1,0:T(8,128)S(1)}, u32[]{:S(2)}, u32[]{:S(2)}) async-start(f32[32,64,256]{2,1,0:T(8,128)} %pick_phases.3), calls=%async_computation.2 | async-start | bytes 4194304 | tf_op jit(solution)/shard_map/all_to_all | solution.py:435
  22.7 0.0 copy-start.6
  22.7 0.0 copy-start.5
  22.7 3.9 %pick_phases.2 = f32[32,64,256]{2,1,0:T(8,128)} custom-call(s32[64]{0:T(128)} %reshape.14.wanted_ref, f32[64,64,256]{2,1,0:T(8,128)} %bitcast.6), custom_call_target="tpu_custom_call" | custom-call | tf_op jit(solution)/shard_map/pick_phases/pallas_call | solution.py:410
  26.6 43.9 %all-to-all-done.2 = f32[32,64,256]{2,1,0:T(8,128)S(1)} async-done(((f32[32,64,256]{2,1,0:T(8,128)}), f32[32,64,256]{2,1,0:T(8,128)S(1)}, u32[]{:S(2)}, u32[]{:S(2)}) %all-to-all-start.2) | async-done | bytes 2097184 | tf_op jit(solution)/shard_map/all_to_all | solution.py:435
  70.5 3.7 %all-to-all-start.1 = ((f32[32,64,256]{2,1,0:T(8,128)}), f32[32,64,256]{2,1,0:T(8,128)}, u32[]{:S(2)}, u32[]{:S(2)}) async-start(f32[32,64,256]{2,1,0:T(8,128)} %pick_phases.2), calls=%async_computation.1 | async-start | bytes 4194304 | tf_op jit(solution)/shard_map/all_to_all | solution.py:435
  74.2 0.6 collective-permute-start.6
  74.8 0.0 copy-done.5
  74.8 2.4 collective-permute-start.7
  77.2 0.5 collective-permute-start.8
  77.8 3.8 %fetch_chunk.1 = (f32[8,64,256]{2,1,0:T(8,128)}, f32[8,64,256]{2,1,0:T(8,128)}, f32[8,64,256]{2,1,0:T(8,128)}, f32[8,64,256]{2,1,0:T(8,128)}) custom-call(s32[64]{0:T(128)} %get-tuple-element.23.order_ref, f32[64,64,256]{2,1,0:T(8,128)} %patches_ref.3), custom_call_target="tpu_custom_call" | custom-call | tf_op jit(solution)/shard_map/fetch_chunk/pallas_call | solution.py:340
  81.6 1.5 collective-permute-start
  83.1 2.0 collective-permute-start.1
  85.1 36.4 %collective-permute-done.6.refs_1_ = f32[8,64,256]{2,1,0:T(8,128)} collective-permute-done((f32[8,64,256]{2,1,0:T(8,128)S(1)}, f32[8,64,256]{2,1,0:T(8,128)}, u32[]{:S(2)}, u32[]{:S(2)}) %collective-permute-start.6) | collective-permute-done | bytes 524320 | tf_op jit(solution)/shard_map/ppermute | solution.py:428
  121.5 2.5 collective-permute-start.2
  124.0 52.3 %collective-permute-done.7.refs_2_ = f32[8,64,256]{2,1,0:T(8,128)} collective-permute-done((f32[8,64,256]{2,1,0:T(8,128)S(1)}, f32[8,64,256]{2,1,0:T(8,128)}, u32[]{:S(2)}, u32[]{:S(2)}) %collective-permute-start.7) | collective-permute-done | bytes 524320 | tf_op jit(solution)/shard_map/ppermute | solution.py:428
  176.3 13.6 %collective-permute-done.8.refs_3_ = f32[8,64,256]{2,1,0:T(8,128)} collective-permute-done((f32[8,64,256]{2,1,0:T(8,128)}, f32[8,64,256]{2,1,0:T(8,128)}, u32[]{:S(2)}, u32[]{:S(2)}) %collective-permute-start.8) | collective-permute-done | bytes 524320 | tf_op jit(solution)/shard_map/ppermute | solution.py:428
  190.0 27.1 %refocus.3 = (f32[8,64,256]{2,1,0:T(8,128)}, f32[8,64,256]{2,1,0:T(8,128)}, f32[8,64,256]{2,1,0:T(8,128)}, f32[8,64,256]{2,1,0:T(8,128)}) custom-call(bf16[4,256,256]{2,1,0:T(8,128)(2,1)} %constant.2.clone.table_ref, f32[8,64,256]{2,1,0:T(8,128)} %get-tuple-element.33.refs_0_, f32[8,64,256]{2,1,0:T(8,128)} %collective-permute-done.6.refs_1_, ...), custom_call_target="tpu_custom_call" | custom-call | tf_op jit(solution)/shard_map/refocus/pallas_call | solution.py:127
  217.1 0.1 collective-permute-start.9
  217.2 1.8 collective-permute-start.10
  219.0 0.0 collective-permute-done.refs_1_
  219.0 1.7 collective-permute-start.11
  220.7 0.0 collective-permute-done.1.refs_2_
  220.7 0.0 collective-permute-done.2.refs_3_
  220.7 0.0 all-to-all-done.1
  220.7 0.8 copy-done.4
  221.6 27.1 %refocus.2 = (f32[8,64,256]{2,1,0:T(8,128)}, f32[8,64,256]{2,1,0:T(8,128)}, f32[8,64,256]{2,1,0:T(8,128)}, f32[8,64,256]{2,1,0:T(8,128)}) custom-call(bf16[4,256,256]{2,1,0:T(8,128)(2,1)} %constant.2.clone.table_ref, f32[8,64,256]{2,1,0:T(8,128)} %get-tuple-element.24.refs_0_, f32[8,64,256]{2,1,0:T(8,128)} %copy-done.3, f32[8,64,256]{2,1,0:T(8,128)} %copy-done.4, ...), custom_call_target="tpu_custom_call" | custom-call | tf_op jit(solution)/shard_map/refocus/pallas_call | solution.py:127
  248.6 1.1 collective-permute-start.3
  249.8 0.8 collective-permute-start.5
  250.5 0.0 collective-permute-done.9.refs_1_
  250.5 1.7 collective-permute-start.4
  252.2 12.9 %collective-permute-done.10.refs_2_ = f32[8,64,256]{2,1,0:T(8,128)S(1)} collective-permute-done((f32[8,64,256]{2,1,0:T(8,128)}, f32[8,64,256]{2,1,0:T(8,128)S(1)}, u32[]{:S(2)}, u32[]{:S(2)}) %collective-permute-start.10) | collective-permute-done | bytes 524320 | tf_op jit(solution)/shard_map/ppermute | solution.py:428
  265.1 24.7 %collective-permute-done.11.refs_3_ = f32[8,64,256]{2,1,0:T(8,128)S(1)} collective-permute-done((f32[8,64,256]{2,1,0:T(8,128)}, f32[8,64,256]{2,1,0:T(8,128)S(1)}, u32[]{:S(2)}, u32[]{:S(2)}) %collective-permute-start.11) | collective-permute-done | bytes 524320 | tf_op jit(solution)/shard_map/ppermute | solution.py:428
  289.8 0.0 copy-done
  289.8 2.2 store_chunk.4.refs_1_
  292.1 1.5 store_chunk.5.refs_1_
  293.6 0.0 collective-permute-done.5.refs_0_
  293.6 1.9 store_chunk.6.refs_2_
  295.6 3.5 %collective-permute-done.3.refs_0_ = f32[8,64,256]{2,1,0:T(8,128)S(1)} collective-permute-done((f32[8,64,256]{2,1,0:T(8,128)}, f32[8,64,256]{2,1,0:T(8,128)S(1)}, u32[]{:S(2)}, u32[]{:S(2)}) %collective-permute-start.3) | collective-permute-done | bytes 524320 | tf_op jit(solution)/shard_map/ppermute | solution.py:428
  299.0 11.2 %collective-permute-done.4.refs_1_ = f32[8,64,256]{2,1,0:T(8,128)} collective-permute-done((f32[8,64,256]{2,1,0:T(8,128)}, f32[8,64,256]{2,1,0:T(8,128)}, u32[]{:S(2)}, u32[]{:S(2)}) %collective-permute-start.4) | collective-permute-done | bytes 524320 | tf_op jit(solution)/shard_map/ppermute | solution.py:428
  310.2 2.1 store_chunk.7
  (9 shorter events, 0.0 us)
Async XLA Ops:
  17.5 53.0 %all-to-all-start.2 = ((f32[32,64,256]{2,1,0:T(8,128)}), f32[32,64,256]{2,1,0:T(8,128)S(1)}, u32[]{:S(2)}, u32[]{:S(2)}) async-start(f32[32,64,256]{2,1,0:T(8,128)} %pick_phases.3), calls=%async_computation.2 | async-start | bytes 4194304 | tf_op jit(solution)/shard_map/all_to_all | solution.py:435
  22.7 51.5 %copy-start.6 = (f32[8,64,256]{2,1,0:T(8,128)S(1)}, f32[8,64,256]{2,1,0:T(8,128)}, u32[]{:S(2)}) copy-start(f32[8,64,256]{2,1,0:T(8,128)} %get-tuple-element.34) | copy-start | bytes 1572868
  22.7 52.2 %copy-start.5 = (f32[8,64,256]{2,1,0:T(8,128)S(1)}, f32[8,64,256]{2,1,0:T(8,128)}, u32[]{:S(2)}) copy-start(f32[8,64,256]{2,1,0:T(8,128)} %get-tuple-element.35) | copy-start | bytes 1572868
  70.5 11.2 %copy-start.2 = (f32[32,64,256]{2,1,0:T(8,128)}, f32[32,64,256]{2,1,0:T(8,128)S(1)}, u32[]{:S(2)}) copy-start(f32[32,64,256]{2,1,0:T(8,128)S(1)} %all-to-all-done.2) | copy-start | bytes 6291460
  70.5 150.2 %all-to-all-start.1 = ((f32[32,64,256]{2,1,0:T(8,128)}), f32[32,64,256]{2,1,0:T(8,128)}, u32[]{:S(2)}, u32[]{:S(2)}) async-start(f32[32,64,256]{2,1,0:T(8,128)} %pick_phases.2), calls=%async_computation.1 | async-start | bytes 4194304 | tf_op jit(solution)/shard_map/all_to_all | solution.py:435
  74.2 47.3 %collective-permute-start.6 = (f32[8,64,256]{2,1,0:T(8,128)S(1)}, f32[8,64,256]{2,1,0:T(8,128)}, u32[]{:S(2)}, u32[]{:S(2)}) collective-permute-start(f32[8,64,256]{2,1,0:T(8,128)S(1)} %copy-done.6), channel_id=1, source_target_pairs={{0,1},{1,0},{2,3},{3,2},{4,5},{5,4},{6,7},{7,6},{8,9},{9,8},{10,11... | collective-permute-start | bytes 1572872 | tf_op jit(solution)/shard_map/ppermute | solution.py:428
  74.8 101.5 %collective-permute-start.7 = (f32[8,64,256]{2,1,0:T(8,128)S(1)}, f32[8,64,256]{2,1,0:T(8,128)}, u32[]{:S(2)}, u32[]{:S(2)}) collective-permute-start(f32[8,64,256]{2,1,0:T(8,128)S(1)} %copy-done.5), channel_id=1, source_target_pairs={{0,2},{1,3},{2,0},{3,1},{4,6},{5,7},{6,4},{7,5},{8,10},{9,11},{10,... | collective-permute-start | bytes 1572872 | tf_op jit(solution)/shard_map/ppermute | solution.py:428
  77.2 112.8 %collective-permute-start.8 = (f32[8,64,256]{2,1,0:T(8,128)}, f32[8,64,256]{2,1,0:T(8,128)}, u32[]{:S(2)}, u32[]{:S(2)}) collective-permute-start(f32[8,64,256]{2,1,0:T(8,128)} %get-tuple-element.36), channel_id=1, source_target_pairs={{0,3},{1,2},{2,1},{3,0},{4,7},{5,6},{6,5},{7,4},{8,11},{9,10},{10,... | collective-permute-start | bytes 1572872 | tf_op jit(solution)/shard_map/ppermute | solution.py:428
  81.6 137.4 %collective-permute-start = (f32[8,64,256]{2,1,0:T(8,128)}, f32[8,64,256]{2,1,0:T(8,128)S(1)}, u32[]{:S(2)}, u32[]{:S(2)}) collective-permute-start(f32[8,64,256]{2,1,0:T(8,128)} %get-tuple-element.25), channel_id=1, source_target_pairs={{0,1},{1,0},{2,3},{3,2},{4,5},{5,4},{6,7},{7,6},{8,9},{9,8},{10,11... | collective-permute-start | bytes 1572872 | tf_op jit(solution)/shard_map/ppermute | solution.py:428
  83.1 137.5 %collective-permute-start.1 = (f32[8,64,256]{2,1,0:T(8,128)}, f32[8,64,256]{2,1,0:T(8,128)S(1)}, u32[]{:S(2)}, u32[]{:S(2)}) collective-permute-start(f32[8,64,256]{2,1,0:T(8,128)} %get-tuple-element.26), channel_id=1, source_target_pairs={{0,2},{1,3},{2,0},{3,1},{4,6},{5,7},{6,4},{7,5},{8,10},{9,11},{10,... | collective-permute-start | bytes 1572872 | tf_op jit(solution)/shard_map/ppermute | solution.py:428
  121.5 99.2 %collective-permute-start.2 = (f32[8,64,256]{2,1,0:T(8,128)}, f32[8,64,256]{2,1,0:T(8,128)}, u32[]{:S(2)}, u32[]{:S(2)}) collective-permute-start(f32[8,64,256]{2,1,0:T(8,128)} %get-tuple-element.27), channel_id=1, source_target_pairs={{0,3},{1,2},{2,1},{3,0},{4,7},{5,6},{6,5},{7,4},{8,11},{9,10},{10,... | collective-permute-start | bytes 1572872 | tf_op jit(solution)/shard_map/ppermute | solution.py:428
  217.1 72.7 %copy-start = (f32[8,64,256]{2,1,0:T(8,128)S(1)}, f32[8,64,256]{2,1,0:T(8,128)}, u32[]{:S(2)}) copy-start(f32[8,64,256]{2,1,0:T(8,128)} %get-tuple-element.37.refs_0_) | copy-start | bytes 1572868
  217.1 33.4 %collective-permute-start.9 = (f32[8,64,256]{2,1,0:T(8,128)}, f32[8,64,256]{2,1,0:T(8,128)S(1)}, u32[]{:S(2)}, u32[]{:S(2)}) collective-permute-start(f32[8,64,256]{2,1,0:T(8,128)} %get-tuple-element.38), channel_id=1, source_target_pairs={{0,1},{1,0},{2,3},{3,2},{4,5},{5,4},{6,7},{7,6},{8,9},{9,8},{10,11... | collective-permute-start | bytes 1572872 | tf_op jit(solution)/shard_map/ppermute | solution.py:428
  217.2 47.9 %collective-permute-start.10 = (f32[8,64,256]{2,1,0:T(8,128)}, f32[8,64,256]{2,1,0:T(8,128)S(1)}, u32[]{:S(2)}, u32[]{:S(2)}) collective-permute-start(f32[8,64,256]{2,1,0:T(8,128)} %get-tuple-element.39), channel_id=1, source_target_pairs={{0,2},{1,3},{2,0},{3,1},{4,6},{5,7},{6,4},{7,5},{8,10},{9,11},{10,... | collective-permute-start | bytes 1572872 | tf_op jit(solution)/shard_map/ppermute | solution.py:428
  219.0 1.7 copy-start.3
  219.0 70.9 %collective-permute-start.11 = (f32[8,64,256]{2,1,0:T(8,128)}, f32[8,64,256]{2,1,0:T(8,128)S(1)}, u32[]{:S(2)}, u32[]{:S(2)}) collective-permute-start(f32[8,64,256]{2,1,0:T(8,128)} %get-tuple-element.40), channel_id=1, source_target_pairs={{0,3},{1,2},{2,1},{3,0},{4,7},{5,6},{6,5},{7,4},{8,11},{9,10},{10,... | collective-permute-start | bytes 1572872 | tf_op jit(solution)/shard_map/ppermute | solution.py:428
  220.7 0.9 copy-start.4
  248.6 43.4 %copy-start.1 = (f32[8,64,256]{2,1,0:T(8,128)S(1)}, f32[8,64,256]{2,1,0:T(8,128)}, u32[]{:S(2)}) copy-start(f32[8,64,256]{2,1,0:T(8,128)} %get-tuple-element.32.refs_0_) | copy-start | bytes 1572868
  248.6 50.4 %collective-permute-start.3 = (f32[8,64,256]{2,1,0:T(8,128)}, f32[8,64,256]{2,1,0:T(8,128)S(1)}, u32[]{:S(2)}, u32[]{:S(2)}) collective-permute-start(f32[8,64,256]{2,1,0:T(8,128)} %get-tuple-element.29), channel_id=1, source_target_pairs={{0,2},{1,3},{2,0},{3,1},{4,6},{5,7},{6,4},{7,5},{8,10},{9,11},{10,... | collective-permute-start | bytes 1572872 | tf_op jit(solution)/shard_map/ppermute | solution.py:428
  249.8 43.9 %collective-permute-start.5 = (f32[8,64,256]{2,1,0:T(8,128)}, f32[8,64,256]{2,1,0:T(8,128)}, u32[]{:S(2)}, u32[]{:S(2)}) collective-permute-start(f32[8,64,256]{2,1,0:T(8,128)} %get-tuple-element.31), channel_id=1, source_target_pairs={{0,1},{1,0},{2,3},{3,2},{4,5},{5,4},{6,7},{7,6},{8,9},{9,8},{10,11... | collective-permute-start | bytes 1572872 | tf_op jit(solution)/shard_map/ppermute | solution.py:428
  250.5 59.7 %collective-permute-start.4 = (f32[8,64,256]{2,1,0:T(8,128)}, f32[8,64,256]{2,1,0:T(8,128)}, u32[]{:S(2)}, u32[]{:S(2)}) collective-permute-start(f32[8,64,256]{2,1,0:T(8,128)} %get-tuple-element.30), channel_id=1, source_target_pairs={{0,3},{1,2},{2,1},{3,0},{4,7},{5,6},{6,5},{7,4},{8,11},{9,10},{10,... | collective-permute-start | bytes 1572872 | tf_op jit(solution)/shard_map/ppermute | solution.py:428
